TPU v7x, 32 devices: a whole 2x2x4 slice. The times are simulated.
32 devices in a mesh: branch: 4 (over x, core), ty: 2 (over y), tx: 4 (over z).
Axes of the slice: x: 2, y: 2, z: 4, core: 2. Of those that a mesh axis runs over, the one named last changes fastest.
Arguments:
- feat0: bfloat16 [48, 128, 256], P(None, 'ty', 'tx'), may hold values from -6 to 6
- feat1: bfloat16 [96, 64, 128], P(None, 'ty', 'tx'), may hold values from -6 to 6
- feat2: bfloat16 [192, 32, 64], P(None, 'ty', 'tx'), may hold values from -6 to 6
- feat3: bfloat16 [384, 16, 32], P(None, 'ty', 'tx'), may hold values from -6 to 6
- block_w0: bfloat16 [2, 48, 432], replicated, may hold values from -0.3125 to 0.3125
- block_w1: bfloat16 [2, 96, 864], replicated, may hold values from -0.21875 to 0.21875
- block_w2: bfloat16 [2, 192, 1728], replicated, may hold values from -0.15625 to 0.15625
- block_w3: bfloat16 [2, 384, 3456], replicated, may hold values from -0.109375 to 0.109375
- block_b0: float32 [2, 48], replicated, may hold values from -1.8 to 1.8
- block_b1: float32 [2, 96], replicated, may hold values from -1.8 to 1.8
- block_b2: float32 [2, 192], replicated, may hold values from -1.8 to 1.8
- block_b3: float32 [2, 384], replicated, may hold values from -1.8 to 1.8
- up_w1: bfloat16 [1, 48, 96], replicated, may hold values from -0.625 to 0.625
- up_w2: bfloat16 [1, 144, 192], replicated, may hold values from -0.4375 to 0.4375
- up_w3: bfloat16 [1, 336, 384], replicated, may hold values from -0.3125 to 0.3125
- down_mid0: bfloat16 [1, 3, 48, 432], replicated, may hold values from -0.3125 to 0.3125
- down_mid1: bfloat16 [1, 1, 96, 864], replicated, may hold values from -0.21875 to 0.21875
- down_fin0: bfloat16 [1, 672, 432], replicated, may hold values from -0.3125 to 0.3125
- down_fin1: bfloat16 [1, 576, 864], replicated, may hold values from -0.21875 to 0.21875
- down_fin2: bfloat16 [1, 384, 1728], replicated, may hold values from -0.15625 to 0.15625
Outputs:
- joined0: bfloat16 [48, 128, 256], P(None, 'ty', 'tx')
- joined1: bfloat16 [96, 64, 128], P(None, 'ty', 'tx')
- joined2: bfloat16 [192, 32, 64], P(None, 'ty', 'tx')
- joined3: bfloat16 [384, 16, 32], P(None, 'ty', 'tx')
All inputs are finite; a program needn't handle non-finite values.
Results may differ from a plain program's by a relative error of at most 0.0095.
Values may be sent and summed in bfloat16 or wider, within the bound.
A program may use at most 128 MiB of HBM per device.

v0:
```python
import functools

import jax
import jax.numpy as jnp
from jax import lax
from jax.experimental import pallas as pl
from jax.experimental.pallas import tpu as pltpu
from jax.sharding import PartitionSpec as P

RIMS = (7, 3, 1, 0)
LANES = 128
NT = (((1,), (1,)), ((), ()))
NN = (((1,), (0,)), ((), ()))
WAYS = [(dy, dx) for dy in (-1, 0, 1) for dx in (-1, 0, 1) if dy or dx]
F32, BF16 = jnp.float32, jnp.bfloat16


def up_to(n, m):
    return -(-n // m) * m


class Level:
    def __init__(self, level, shape):
        self.rows, self.cols, self.chan = shape
        self.rim = RIMS[level]
        self.low = self.rim + 2
        self.pitch = up_to(self.cols + 2 + self.low, 8)
        self.lead = self.low + 1
        self.tail = self.pitch - self.cols
        self.planes = up_to(self.chan, LANES) // LANES
        self.near = up_to(self.low, 8)
        self.total = (self.lead + self.rows + 4) * self.pitch

    def at(self, row, col=0):
        return (row + self.lead) * self.pitch + col

    def first(self):
        start = self.at(-self.rim - 1) - self.tail
        return start, self.at(self.rows) + self.cols + 8 - start

    def second(self):
        start = self.at(-self.rim) - self.tail
        return start, self.at(self.rows - 1) + self.cols - start


def source_of(lv, way):
    dy, dx = way
    rows = (0, lv.rows) if dy == 0 else ((lv.rows - lv.low, lv.low) if dy > 0 else (0, 2))
    cols = (0, lv.cols) if dx == 0 else ((lv.cols - lv.near, lv.near) if dx > 0 else (0, 8))
    return rows, cols


def on_map(way, side):
    ok = True
    for step, axis in zip(way, ("ty", "tx")):
        if step:
            place = lax.axis_index(axis) + side * step
            ok = ok & (place >= 0) & (place < lax.axis_size(axis))
    return ok


def exchange(levels, *refs):
    feats, outs, (send, recv) = refs[:4], refs[4:36], refs[36:]
    here = {a: lax.axis_index(a) for a in ("ty", "tx")}
    barrier = pltpu.get_barrier_semaphore()

    def there(way):
        return {"ty": here["ty"] + way[0], "tx": here["tx"] + way[1]}

    count = 0
    for way in WAYS:
        ok = on_map(way, 1)

        @pl.when(ok)
        def _(way=way):
            pl.semaphore_signal(barrier, 1, device_id=there(way))

        count = count + jnp.where(ok, 1, 0)
    pl.semaphore_wait(barrier, count)

    def copy(l, k):
        way = WAYS[k]
        (r, nr), (c, nc) = source_of(levels[l], way)
        return pltpu.make_async_remote_copy(
            feats[l].at[pl.ds(r, nr), pl.ds(c, nc)],
            outs[8 * l + k],
            send.at[8 * l + k],
            recv.at[8 * l + k],
            device_id=there(way),
        )

    for k, way in enumerate(WAYS):

        @pl.when(on_map(way, 1))
        def _(k=k):
            for l in range(4):
                copy(l, k).start()

    for k, way in enumerate(WAYS):

        @pl.when(on_map(way, 1))
        def _(k=k):
            for l in range(4):
                copy(l, k).wait_send()

        @pl.when(on_map(way, -1))
        def _(k=k):
            for l in range(4):
                copy(l, k).wait_recv()


def halos_of(levels, feats):
    shapes = []
    for lv in levels:
        for way in WAYS:
            (_, nr), (_, nc) = source_of(lv, way)
            shapes.append(jax.ShapeDtypeStruct((nr, nc, lv.chan), BF16))
    hbm = pl.BlockSpec(memory_space=pl.ANY)
    return pl.pallas_call(
        functools.partial(exchange, levels),
        out_shape=shapes,
        in_specs=[hbm] * 4,
        out_specs=[hbm] * 32,
        scratch_shapes=[pltpu.SemaphoreType.DMA((32,))] * 2,
        compiler_params=pltpu.CompilerParams(collective_id=0, has_side_effects=True),
    )(*feats)


def chunking(length, most):
    n = -(-length // most)
    return n, up_to(-(-length // n), 16)


def body(levels, *refs):
    refs = list(refs)

    def take(n):
        out = refs[:n]
        del refs[:n]
        return out

    feats, halos = take(4), take(32)
    w0, w1, w2_hbm, w3_hbm = take(4)
    biases = take(4)
    up1, up2, up3, wd0, wd1a, wd1v, wd2_hbm = take(7)
    outs = take(4)
    xs, hs = take(4), take(4)
    spread, odd, cols2, cols3 = take(4)
    w2, w3, wd2 = take(3)
    t01, v0, t2, v1, u0, u1, u2 = take(7)
    (sems,) = take(1)
    l0, l1, l2, l3 = levels
    copies = [
        pltpu.make_async_copy(a, b, sems.at[i])
        for i, (a, b) in enumerate(((w2_hbm, w2), (w3_hbm, w3), (wd2_hbm, wd2)))
    ]
    for c in copies:
        c.start()

    ty, tx = lax.axis_index("ty"), lax.axis_index("tx")
    top, bottom = ty == 0, ty == lax.axis_size("ty") - 1
    left, right = tx == 0, tx == lax.axis_size("tx") - 1

    def lane(shape):
        return lax.broadcasted_iota(jnp.int32, shape, len(shape) - 1)

    def rows_loop(n, run):
        def step(i, _):
            run(i)
            return 0

        lax.fori_loop(0, n, step, 0)

    def put(l, at, value):
        lv = levels[l]
        for p in range(lv.planes):
            w = min(LANES, lv.chan - p * LANES)
            xs[l][p, pl.ds(at, value.shape[0]), 0:w] = value[:, p * LANES : p * LANES + w]

    for l, lv in enumerate(levels):
        xs[l][...] = jnp.zeros_like(xs[l])
    for ref in (v0, v1):
        ref[...] = jnp.zeros_like(ref)
    for l, lv in enumerate(levels):

        def place(source, row, col, l=l, lv=lv, skip=0, keep=None):
            def run(i):
                at = pl.multiple_of((i + row + lv.lead) * lv.pitch + col, 8)
                put(l, at + skip, source[i].astype(F32)[skip:keep])

            rows_loop(source.shape[0], run)

        place(feats[l], 0, 0)
        for k, way in enumerate(WAYS):
            dy, dx = way
            row = {0: 0, 1: -lv.low, -1: lv.rows}[dy]
            col, skip, keep = {0: (0, 0, None), 1: (-lv.near, lv.near - lv.low, None), -1: (lv.cols, 0, 2)}[dx]

            @pl.when(on_map(way, -1))
            def _(k=k, row=row, col=col, skip=skip, keep=keep):
                place(halos[8 * l + k], row, col, skip=skip, keep=keep)

    def blank(ref, lv, low, high):
        planes = ref.shape[0]

        def columns(col, n):
            start = lv.at(-low - 1)
            count = low + 1 + lv.rows + high
            for c in range(col, col + n):
                for p in range(planes):
                    ref[p, pl.ds(start + c, count, stride=lv.pitch), :] = jnp.zeros((count, LANES), F32)

        def rows(row, n):
            for p in range(planes):
                size = n * lv.pitch
                ref[p, pl.ds(lv.at(row) - lv.tail + 2, size), :] = jnp.zeros((size, LANES), F32)

        pl.when(left)(lambda: columns(lv.pitch - low, low))
        if high:
            pl.when(right)(lambda: columns(lv.cols, high))
            pl.when(bottom)(lambda: rows(lv.rows, high))

        pl.when(top)(lambda: rows(-low, low))

    def wide_conv(l, src, dst, weight, bias, span, residual):
        lv = levels[l]
        start, length = span
        n, m = chunking(length, 656)
        C = lv.chan

        def run(i):
            base = pl.multiple_of(start + i * m, 8)
            a, b, c = (
                src[0, pl.ds(pl.multiple_of(base - 8 + d * lv.pitch, 8), m + 16), :] for d in (-1, 0, 1)
            )
            if 3 * C <= 2 * LANES:
                ids = lane(a.shape)
                moved = pltpu.roll(c, 2 * C, 1)
                tile0 = a + pltpu.roll(b, C, 1) + jnp.where(ids >= 2 * C, moved, 0.0)
                tile1 = jnp.where(ids < 3 * C - LANES, moved, 0.0)
                lhs = jnp.concatenate([tile0.astype(BF16), tile1.astype(BF16)], axis=1)
            else:
                lhs = jnp.concatenate([a.astype(BF16), b.astype(BF16), c.astype(BF16)], axis=1)
            o = lax.dot_general(lhs, weight[...], NT, preferred_element_type=F32)
            for q in range(3):
                spread[q, 0 : m + 16, :] = o[:, q * LANES : (q + 1) * LANES]
            y = spread[0, 7 : 7 + m, :] + spread[1, 8 : 8 + m, :] + spread[2, 9 : 9 + m, :]
            y = y + bias
            if residual:
                y = y + dst[0, pl.ds(base, m), :]
            dst[0, pl.ds(base, m), :] = jnp.maximum(y, 0.0)

        rows_loop(n, run)

    def offset(lv, t):
        return (t // 3 - 1) * lv.pitch + t % 3 - 1

    def deep_conv2(src, dst, weight, bias, span, residual):
        lv = l2
        start, length = span
        m = up_to(length, 16)
        total = lv.total
        p0, p1 = src[0, :, :], src[1, :, :]
        ids = lane((total, LANES))
        r0, r1 = pltpu.roll(p0, 64, 1), pltpu.roll(p1, 64, 1)
        odd[0, :, :] = jnp.where(ids >= 64, r0, 0.0)
        odd[1, :, :] = jnp.where(ids < 64, r0, r1)

        def piece(ref, p, t):
            return ref[p, pl.ds(start + offset(lv, t), m), :]

        for t in range(0, 9, 2):
            k = 3 * (t // 2) * LANES
            cols2[0:m, k : k + 128] = piece(src, 0, t).astype(BF16)
            tile = piece(src, 1, t)
            if t == 8:
                cols2[0:m, k + 128 : k + 192] = tile[:, 0:64].astype(BF16)
            else:
                cols2[0:m, k + 128 : k + 256] = (tile + piece(odd, 0, t + 1)).astype(BF16)
                cols2[0:m, k + 256 : k + 384] = piece(odd, 1, t + 1).astype(BF16)
        y = lax.dot_general(cols2[0:m, :], weight, NT, preferred_element_type=F32) + bias[:, 0 : lv.chan]
        for p in range(2):
            w = min(LANES, lv.chan - p * LANES)
            part = y[:, p * LANES : p * LANES + w]
            if residual:
                part = part + dst[p, pl.ds(start, m), 0:w]
            dst[p, pl.ds(start, m), 0:w] = jnp.maximum(part, 0.0)

    def deep_conv3(src, dst, weight, bias, span, residual):
        lv = l3
        start, length = span
        m = up_to(length, 16)
        for t in range(9):
            for p in range(lv.planes):
                k = (t * lv.planes + p) * LANES
                cols3[0:m, k : k + LANES] = src[p, pl.ds(start + offset(lv, t), m), :].astype(BF16)
        y = lax.dot_general(cols3[0:m, :], weight, NT, preferred_element_type=F32) + bias
        for p in range(lv.planes):
            part = y[:, p * LANES : (p + 1) * LANES]
            if residual:
                part = part + dst[p, pl.ds(start, m), :]
            dst[p, pl.ds(start, m), :] = jnp.maximum(part, 0.0)

    for l in (0, 1):
        lv = levels[l]
        wide_conv(l, xs[l], hs[l], (w0, w1)[l].at[0], biases[l][0:1, :], lv.first(), False)
        blank(hs[l], lv, lv.rim + 1, 1)
        wide_conv(l, hs[l], xs[l], (w0, w1)[l].at[1], biases[l][1:2, :], lv.second(), True)
        blank(xs[l], lv, lv.rim, 0)

    hs[2][1, :, :] = jnp.zeros((l2.total, LANES), F32)
    copies[0].wait()
    deep_conv2(xs[2], hs[2], w2[0], biases[2][0:1, :], l2.first(), False)
    blank(hs[2], l2, l2.rim + 1, 1)
    deep_conv2(hs[2], xs[2], w2[1], biases[2][1:2, :], l2.second(), True)
    blank(xs[2], l2, l2.rim, 0)
    copies[1].wait()
    deep_conv3(xs[3], hs[3], w3[0], biases[3][0:1, :], l3.first(), False)
    blank(hs[3], l3, 1, 1)
    deep_conv3(hs[3], xs[3], w3[1], biases[3][1:2, :], l3.second(), True)

    def gathered(src, plane, big, small, i, t, width=None):
        width = small.pitch if width is None else width
        at = (2 * i + t // 3 - 1 + big.lead) * big.pitch + 2 * (small.cols - width) + t % 3 - 1
        return src[plane, pl.ds(at, width, stride=2), :]

    rim = RIMS[1]
    rows = up_to(rim + l1.rows, 4)

    def down0(k):
        i0 = l1.rows - rows + 4 * k
        taps = [
            jnp.concatenate([gathered(xs[0], 0, l0, l1, i0 + r, t) for r in range(4)], axis=0).astype(BF16)
            for t in range(9)
        ]
        o = lax.dot_general(jnp.concatenate(taps, axis=1), wd0[...], NT, preferred_element_type=F32)
        at = pl.multiple_of((i0 + l1.lead) * l1.pitch - l1.tail, 8)
        t01[0, pl.ds(at, 4 * l1.pitch), :] = o[:, 0:LANES]
        v0[0, pl.ds(at, 4 * l1.pitch), :] = jnp.maximum(o[:, LANES:], 0.0)

    rows_loop(rows // 4, down0)
    blank(v0, l1, rim, 0)

    rows = l2.rows + 2
    at = l2.at(-2) - l2.tail
    span = rows * l2.pitch

    def down1(src, weight):
        taps = [
            jnp.concatenate([gathered(src, 0, l1, l2, i, t) for i in range(-2, l2.rows)], axis=0).astype(BF16)
            for t in range(9)
        ]
        return lax.dot_general(jnp.concatenate(taps, axis=1), weight[...], NT, preferred_element_type=F32)

    o = down1(xs[1], wd1a)
    e = down1(v0, wd1v)
    second = o[:, LANES : 2 * LANES] + e[:, LANES : 2 * LANES]
    ids = lane(second.shape)
    t2[0, 0:span, :] = o[:, 0:LANES] + e[:, 0:LANES]
    t2[1, 0:span, :] = second
    v1[0, pl.ds(at, span), :] = jnp.where(ids >= 64, jnp.maximum(second, 0.0), 0.0)
    v1[1, pl.ds(at, span), :] = jnp.maximum(o[:, 2 * LANES :], 0.0)
    blank(v1, l2, 1, 0)
    taps = []
    for t in range(9):
        for p in range(3):
            parts = []
            for i in range(l3.rows):
                piece = gathered(xs[2] if p < 2 else v1, p if p < 2 else 1, l2, l3, i, t, l3.cols)
                if p == 1:
                    piece = piece + gathered(v1, 0, l2, l3, i, t, l3.cols)
                parts.append(piece)
            taps.append(jnp.concatenate(parts, axis=0).astype(BF16))
    copies[2].wait()
    t3 = lax.dot_general(jnp.concatenate(taps, axis=1), wd2[...], NN, preferred_element_type=F32)

    def center(l, i):
        lv = levels[l]
        parts = [xs[l][p, pl.ds(lv.at(i), lv.cols), :] for p in range(lv.planes)]
        return jnp.concatenate(parts, axis=1)[:, : lv.chan] if lv.planes > 1 else parts[0][:, : lv.chan]

    a3 = jnp.concatenate([center(3, i) for i in range(l3.rows)], axis=0)
    y3 = jnp.maximum(a3 + t3, 0.0).astype(BF16)
    for i in range(l3.rows):
        outs[3][i, :, :] = y3[i * l3.cols : (i + 1) * l3.cols, :]

    c0, c1, c2 = l0.chan, l1.chan, l2.chan
    a3 = a3.astype(BF16)
    up3_0 = lax.dot_general(a3, up3[0:c0, :], NT, preferred_element_type=F32)
    up3_1 = lax.dot_general(a3, up3[c0 : c0 + c1, :], NT, preferred_element_type=F32)
    up3_2 = lax.dot_general(a3, up3[c0 + c1 :, :], NT, preferred_element_type=F32)

    def enlarge(value, dst, plane, width, rows, cols):
        for i in range(rows):
            line = value[i * cols : (i + 1) * cols, :]
            for di in range(2):
                for dj in range(2):
                    base = (2 * i + di) * 2 * cols + dj
                    dst[plane, pl.ds(base, cols, stride=2), 0:width] = line

    enlarge(up3_0, u2, 0, c0, l3.rows, l3.cols)
    enlarge(up3_1, u2, 1, c1, l3.rows, l3.cols)
    enlarge(up3_2[:, 0:LANES], u2, 2, LANES, l3.rows, l3.cols)
    enlarge(up3_2[:, LANES:], u2, 3, c2 - LANES, l3.rows, l3.cols)
    a2 = jnp.concatenate([center(2, i) for i in range(l2.rows)], axis=0)
    a2b = a2.astype(BF16)
    up2_0 = lax.dot_general(a2b, up2[0:c0, :], NT, preferred_element_type=F32) + u2[0, :, 0:c0]
    up2_1 = lax.dot_general(a2b, up2[c0:, :], NT, preferred_element_type=F32) + u2[1, :, 0:c1]
    for i in range(l2.rows):
        for p in range(2):
            w = min(LANES, c2 - p * LANES)
            line = xs[2][p, pl.ds(l2.at(i), l2.cols), 0:w]
            line = line + t2[p, pl.ds((i + 2) * l2.pitch + l2.tail, l2.cols), 0:w]
            line = line + u2[2 + p, pl.ds(i * l2.cols, l2.cols), 0:w]
            outs[2][i, :, p * LANES : p * LANES + w] = jnp.maximum(line, 0.0).astype(BF16)
    enlarge(up2_0, u1, 0, c0, l2.rows, l2.cols)
    enlarge(up2_1, u1, 1, c1, l2.rows, l2.cols)

    def join1(k):
        lines = []
        for r in range(4):
            i = 4 * k + r
            at = pl.multiple_of((i + l1.lead) * l1.pitch, 8)
            line = xs[1][0, pl.ds(at, l1.cols), 0:c1]
            lines.append(line)
            total = line + t01[0, pl.ds(at, l1.cols), 0:c1]
            total = total + u1[1, pl.ds(pl.multiple_of(i * l1.cols, 8), l1.cols), 0:c1]
            outs[1][i, :, :] = jnp.maximum(total, 0.0).astype(BF16)
        a1 = jnp.concatenate(lines, axis=0).astype(BF16)
        n = 4 * l1.cols
        y = lax.dot_general(a1, up1[...], NT, preferred_element_type=F32)
        y = y + u1[0, pl.ds(pl.multiple_of(k * n, 8), n), 0:c0]
        for r in range(4):
            line = y[r * l1.cols : (r + 1) * l1.cols, :]
            for dj in range(2):
                u0[0, pl.ds(dj, l1.cols, stride=2), 0:c0] = line
            up = u0[0, 0 : l0.cols, 0:c0]
            for di in range(2):
                i = 2 * (4 * k + r) + di
                at = pl.multiple_of((i + l0.lead) * l0.pitch, 8)
                total = xs[0][0, pl.ds(at, l0.cols), 0:c0] + up
                outs[0][i, :, :] = jnp.maximum(total, 0.0).astype(BF16)

    rows_loop(l1.rows // 4, join1)


def spread_out(w, lanes):
    n = w.shape[0]
    w = w.reshape(n, 9, -1)
    return jnp.pad(w, ((0, 0), (0, 0), (0, lanes - w.shape[2])))


def tall(w, n):
    return jnp.pad(w, ((0, n - w.shape[0]),) + ((0, 0),) * (w.ndim - 1))


def per_device(*args):
    feats, weights, biases, rest = args[0:4], args[4:8], args[8:12], args[12:20]
    feats = [f.transpose(1, 2, 0) for f in feats]
    levels = [Level(l, f.shape) for l, f in enumerate(feats)]
    l0, l1, l2, l3 = levels
    c0, c1, c2, c3 = (lv.chan for lv in levels)
    halos = halos_of(levels, feats)
    up1, up2, up3, mid0, mid1, fin0, fin1, fin2 = (r[0] for r in rest)

    def wide(w, c, deep):
        w = w.reshape(2, c, 3, 3, c)
        if 3 * c > 2 * LANES:
            w = jnp.pad(w, ((0, 0),) * 4 + ((0, LANES - c),))
        w = jnp.pad(w, ((0, 0), (0, LANES - c)) + ((0, 0),) * 3)
        w = w.transpose(0, 3, 1, 2, 4).reshape(2, 3 * LANES, -1)
        return jnp.pad(w, ((0, 0), (0, 0), (0, deep - w.shape[2])))

    w0 = wide(weights[0], c0, 2 * LANES)
    w1 = wide(weights[1], c1, 3 * LANES)
    bs = [jnp.pad(b, ((0, 0), (0, up_to(b.shape[1], LANES) - b.shape[1]))) for b in biases]
    wd0 = jnp.concatenate(
        [
            tall(spread_out(fin0[:c1], LANES), LANES),
            tall(spread_out(mid0[0:2].reshape(2 * c0, -1), LANES), LANES),
        ]
    ).reshape(2 * LANES, -1)
    wd1a = jnp.concatenate(
        [tall(spread_out(fin1[:c2], LANES), 2 * LANES), tall(spread_out(mid1[0], LANES), LANES)]
    ).reshape(3 * LANES, -1)
    late = jnp.pad(spread_out(mid0[2], c0), ((0, 0), (0, 0), (c0, 0)))
    wd1v = tall(
        jnp.concatenate([spread_out(fin0[c1 : c1 + c2], 2 * c0), late]), 2 * LANES
    )
    wd1v = jnp.pad(wd1v, ((0, 0), (0, 0), (0, LANES - 2 * c0))).reshape(2 * LANES, -1)

    def deep(w, pad):
        w = w.T.reshape(9, -1, c3)
        return jnp.pad(w, ((0, 0), (0, pad - w.shape[1]), (0, 0)))

    wd2 = jnp.concatenate(
        [deep(fin2, c2), deep(fin0[c1 + c2 :], 64), deep(fin1[c2:], LANES)], axis=1
    ).reshape(-1, c3)

    vmem, any_ = pl.BlockSpec(memory_space=pltpu.VMEM), pl.BlockSpec(memory_space=pl.ANY)
    V = pltpu.VMEM
    maps = [V((lv.planes, lv.total, LANES), F32) for lv in levels]
    m2, m3 = up_to(l2.first()[1], 16), up_to(l3.first()[1], 16)
    n1 = max(chunking(s[1], 656)[1] for lv in levels[:2] for s in (lv.first(), lv.second()))
    scratch = maps * 2 + [
        V((3, n1 + 16, LANES), F32),
        V((2, l2.total, LANES), F32),
        V((m2, 9 * c2), BF16),
        V((m3, 9 * c3), BF16),
        V(weights[2].shape, BF16),
        V(weights[3].shape, BF16),
        V(wd2.shape, BF16),
        V((1, l1.total, LANES), F32),
        V((1, l1.total, LANES), F32),
        V((2, (l2.rows + 2) * l2.pitch, LANES), F32),
        V((2, l2.total, LANES), F32),
        V((1, l0.cols, LANES), F32),
        V((2, l1.rows * l1.cols, LANES), F32),
        V((4, l2.rows * l2.cols, LANES), F32),
        pltpu.SemaphoreType.DMA((3,)),
    ]
    outs = pl.pallas_call(
        functools.partial(body, levels),
        out_shape=[jax.ShapeDtypeStruct(f.shape, BF16) for f in feats],
        in_specs=[vmem] * 36 + [vmem] * 2 + [any_] * 2 + [vmem] * 4 + [vmem] * 6 + [any_],
        out_specs=[vmem] * 4,
        scratch_shapes=scratch,
        compiler_params=pltpu.CompilerParams(vmem_limit_bytes=60 * 2**20),
    )(*feats, *halos, w0, w1, weights[2], weights[3], *bs, up1, up2, up3, wd0, wd1a, wd1v, wd2)
    return tuple(o.transpose(2, 0, 1) for o in outs)


def solution(mesh):
    tiled = P(None, "ty", "tx")
    return jax.shard_map(
        per_device,
        mesh=mesh,
        in_specs=(tiled,) * 4 + (P(),) * 16,
        out_specs=(tiled,) * 4,
        check_vma=False,
    )
```

profile of v0, /device:TPU:22, one launch (start us, length us, event | category | flops | bytes accessed | tf_op | source)
XLA Modules:
  0.0 72.6 jit_solution(14897057845314102196)
XLA Ops:
  0.6 0.0 copy-start.2
  0.6 1.2 %pad.85.refs_40_ = f32[2,128]{1,0:T(2,128)} pad(f32[2,48]{1,0:T(2,128)} %param.28, f32[]{:T(128)} %constant.4.clone.1), padding=0_0x0_80 | pad | bytes 1412 | tf_op jit(solution)/shard_map/jit(_pad)/pad | solution.py:476
  1.9 1.3 %pad.86.refs_41_ = f32[2,128]{1,0:T(2,128)} pad(f32[2,96]{1,0:T(2,128)} %param.29, f32[]{:T(128)} %constant.4.clone.1), padding=0_0x0_32 | pad | bytes 1796 | tf_op jit(solution)/shard_map/jit(_pad)/pad | solution.py:476
  3.2 1.3 %pad.87.refs_42_ = f32[2,256]{1,0:T(2,128)} pad(f32[2,192]{1,0:T(2,128)} %param.30, f32[]{:T(128)} %constant.4.clone.1), padding=0_0x0_64 | pad | bytes 3588 | tf_op jit(solution)/shard_map/jit(_pad)/pad | solution.py:476
  4.4 0.8 %slice.36 = bf16[1,1,48,432]{3,2,1,0:T(8,128)(2,1)S(1)} slice(bf16[1,3,48,432]{3,2,1,0:T(8,128)(2,1)} %param.35), slice={[0:1], [2:3], [0:48], [0:432]} | slice | bytes 82944 | tf_op jit(solution)/shard_map/slice | solution.py:486
  5.2 0.1 copy.46
  5.4 0.9 %slice.33 = bf16[1,2,48,432]{3,2,1,0:T(8,128)(2,1)S(1)} slice(bf16[1,3,48,432]{3,2,1,0:T(8,128)(2,1)} %param.35), slice={[0:1], [0:2], [0:48], [0:432]} | slice | bytes 165888 | tf_op jit(solution)/shard_map/slice | solution.py:480
  6.3 0.2 copy.36
  6.4 0.1 reshape_reshape.3
  6.6 1.1 %copy.38 = bf16[1,1,96,864]{2,3,1,0:T(8,128)(2,1)S(1)} copy(bf16[1,1,96,864]{3,2,1,0:T(8,128)(2,1)} %param.36) | data formatting | bytes 331776 | tf_op args[16]
  7.7 0.0 slice-start
  7.7 1.1 %slice.35 = bf16[1,192,432]{1,2,0:T(8,128)(2,1)S(1)} slice(bf16[1,672,432]{1,2,0:T(8,128)(2,1)} %param.37), slice={[0:1], [96:288], [0:432]} | slice | bytes 331776 | tf_op jit(solution)/shard_map/slice | solution.py:488
  8.8 0.1 fusion.13
  9.0 0.1 pad.122
  9.0 1.1 %copy.43.refs_49_ = bf16[256,1152]{1,0:T(8,128)(2,1)} copy(bf16[256,1152]{0,1:T(8,128)(2,1)S(1)} %bitcast.49) | data formatting | bytes 1179648 | tf_op jit(solution)/shard_map/reshape | solution.py:490
  10.1 0.0 copy-done.2
  10.1 0.2 reshape.62
  10.3 0.0 slice-start.2
  10.4 1.2 %slice.37 = bf16[1,384,432]{1,2,0:T(8,128)(2,1)S(1)} slice(bf16[1,672,432]{1,2,0:T(8,128)(2,1)} %param.37), slice={[0:1], [288:672], [0:432]} | slice | bytes 663552 | tf_op jit(solution)/shard_map/slice | solution.py:497
  11.6 0.0 slice-done
  11.6 0.2 copy.45
  11.8 0.0 copy-start.1
  11.8 0.1 fusion.9
  12.0 1.5 %copy.42.refs_48_ = bf16[384,1152]{1,0:T(8,128)(2,1)} copy(bf16[384,1152]{0,1:T(8,128)(2,1)S(1)} %bitcast.47) | data formatting | bytes 1769472 | tf_op jit(solution)/shard_map/reshape | solution.py:485
  13.5 0.0 slice-done.2
  13.5 0.1 fusion.12
  13.6 1.1 %copy.41.refs_47_ = bf16[256,1152]{1,0:T(8,128)(2,1)} copy(bf16[256,1152]{0,1:T(8,128)(2,1)S(1)} %bitcast.50) | data formatting | bytes 1179648 | tf_op jit(solution)/shard_map/reshape | solution.py:482
  14.6 0.0 copy-done.1
  14.6 0.3 copy.34
  14.9 0.1 pad_bitcast_fusion.1
  15.0 0.6 copy.35
  15.6 1.2 %reshape.65.refs_37_ = bf16[2,384,384]{2,1,0:T(8,128)(2,1)} reshape(bf16[2,3,128,3,128]{4,3,2,1,0:T(4,128)(2,1)S(1)} %copy.35) | data formatting | bytes 1179648 | tf_op jit(solution)/shard_map/reshape | solution.py:471
  16.9 0.0 slice-start.1
  16.9 0.3 pad_bitcast_fusion
  17.2 0.5 copy.32
  17.7 0.2 reshape.63
  17.9 0.2 copy.33
  18.1 0.8 %pad.82.refs_36_ = bf16[2,384,256]{2,1,0:T(8,128)(2,1)} pad(bf16[2,384,144]{2,1,0:T(8,128)(2,1)S(1)} %copy.33, bf16[]{:T(256)} %constant.3.clone.1), padding=0_0x0_0x0_112 | pad | bytes 614402 | tf_op jit(solution)/shard_map/jit(_pad)/pad | solution.py:472
  18.9 0.0 slice-done.1
  18.9 0.0 copy-start
  18.9 0.3 copy.47
  19.2 2.7 %copy.31 = bf16[48,64,64]{0,2,1:T(8,128)(2,1)} copy(bf16[48,64,64]{2,1,0:T(8,128)(2,1)} %param.20) | data formatting | bytes 786432 | tf_op args[0]
  22.0 15.2 %shard_map.219 = (bf16[2,8,48]{2,1,0:T(8,128)(2,1)}, bf16[2,64,48]{2,1,0:T(8,128)(2,1)}, bf16[2,16,48]{2,1,0:T(8,128)(2,1)}, bf16[64,8,48]{2,1,0:T(8,128)(2,1)},...) custom-call(bf16[64,64,48]{2,1,0:T(8,128)(2,1)} %bitcast.45, ...), custom_call_target="tpu_custom_call" | custom-call | tf_op jit(solution)/shard_map/pallas_call | solution.py:119
  37.2 0.0 copy-done
  37.2 2.8 %fusion.4 = bf16[9,384,384]{2,1,0:T(8,128)(2,1)} fusion(bf16[9,96,384]{2,1,0:T(8,128)(2,1)S(1)} %bitcast.48, bf16[9,48,384]{2,1,0:T(8,128)(2,1)S(1)} %bitcast.54, bf16[9,192,384]{2,1,0:T(8,128)(2,1)S(1)} %bitcast.53), kind=kLoop, calls=%fused_computation.7 | loop fusion | flops 15925248 | bytes 4976640 | tf_op jit(solution)/shard_map/concatenate | solution.py:496
  40.0 29.7 %shard_map.220 = (bf16[64,64,48]{2,1,0:T(8,128)(2,1)}, bf16[32,32,96]{2,1,0:T(8,128)(2,1)}, bf16[16,16,192]{2,1,0:T(8,128)(2,1)}, bf16[8,8,384]{2,1,0:T(8,128)(2,1)}) custom-call(bf16[64,64,48]{2,1,0:T(8,128)(2,1)} %bitcast.46, bf16[32,32,96]{2,1,0:T(8,128)(2,1)} %bitcast.56, bf16[16,16,192]{2,1,0:T(8,128)(2,1)} %bitcast.62, bf16[8,8,384]{2,1,0:T(8,128)(2,1)} %bitcast.66, ...), custom_call_target="tpu_custom_call" | custom-call | tf_op jit(solution)/shard_map/pallas_call | solution.py:522
  69.7 2.9 %copy.44 = bf16[48,64,64]{2,1,0:T(8,128)(2,1)} copy(bf16[48,64,64]{0,2,1:T(8,128)(2,1)} %bitcast.57) | data formatting | bytes 786432
Async XLA Ops:
  0.6 9.5 %copy-start.2 = (bf16[2,48,432]{2,1,0:T(8,128)(2,1)S(1)}, bf16[2,48,432]{2,1,0:T(8,128)(2,1)}, u32[]{:S(2)}) copy-start(bf16[2,48,432]{2,1,0:T(8,128)(2,1)} %param.24) | copy-start | bytes 248836
  7.7 3.9 %slice-start = ((bf16[1,576,864]{2,1,0:T(8,128)(2,1)}), bf16[1,192,864]{2,1,0:T(8,128)(2,1)S(1)}, s32[]{:S(2)}) async-start(bf16[1,576,864]{2,1,0:T(8,128)(2,1)} %param.38), calls=%async_computation | async-start | bytes 688128 | tf_op jit(solution)/shard_map/slice | solution.py:484
  10.3 3.2 %slice-start.2 = ((bf16[1,672,432]{1,2,0:T(8,128)(2,1)}), bf16[1,96,432]{1,2,0:T(8,128)(2,1)S(1)}, s32[]{:S(2)}) async-start(bf16[1,672,432]{1,2,0:T(8,128)(2,1)} %param.37), calls=%async_computation.2 | async-start | bytes 221184 | tf_op jit(solution)/shard_map/slice | solution.py:479
  11.8 2.8 %copy-start.1 = (bf16[2,96,864]{2,1,0:T(8,128)(2,1)S(1)}, bf16[2,96,864]{2,1,0:T(8,128)(2,1)}, u32[]{:S(2)}) copy-start(bf16[2,96,864]{2,1,0:T(8,128)(2,1)} %param.25) | copy-start | bytes 995332
  16.9 2.0 %slice-start.1 = ((bf16[1,576,864]{2,1,0:T(8,128)(2,1)}), bf16[1,384,864]{2,1,0:T(8,128)(2,1)S(1)}, s32[]{:S(2)}) async-start(bf16[1,576,864]{2,1,0:T(8,128)(2,1)} %param.38), calls=%async_computation.1 | async-start | bytes 1376256 | tf_op jit(solution)/shard_map/slice | solution.py:497
  18.9 18.3 %copy-start = (bf16[1,384,1728]{1,2,0:T(8,128)(2,1)S(1)}, bf16[1,384,1728]{1,2,0:T(8,128)(2,1)}, u32[]{:S(2)}) copy-start(bf16[1,384,1728]{1,2,0:T(8,128)(2,1)} %param.39) | copy-start | bytes 3981316
where the time goes:
time: 72.9 us; the launch traced here: 72.6 us
  Pallas kernels  44.9 us (62%)
  local copies, waits for them, and re-layouts  23.8 us (33%)
  other arithmetic  3.09 us (4%)
  between operations  0.81 us (1%)
    pallas_call x1, Pallas kernels, per_device(): pl.pallas_call(functools.partial(body, levels), out_shape=[jax.ShapeDtype...  29.7 us
    pallas_call x1, Pallas kernels, halos_of(): pl.pallas_call(functools.partial(exchange, levels), out_shape=shapes, in_...  15.2 us
    unnamed x13, local copies, waits for them, and re-layouts  7.66 us
    pad x3, local copies, waits for them, and re-layouts, per_device(): jnp.pad(b, ((0, 0), (0, up_to(b.shape[1], LANES) - b.shape[1])))  3.79 us
    concatenate x1, other arithmetic, per_device(): jnp.concatenate([deep(fin2, c2), deep(fin0[c1 + c2:], 64), deep(fin1[c2:]...  2.77 us
    reshape x3, local copies, waits for them, and re-layouts, wide(): w = w.transpose(0, 3, 1, 2, 4).reshape(2, 3 * LANES, -1)  1.62 us
    reshape x1, local copies, waits for them, and re-layouts, per_device(): wd1a = jnp.concatenate([tall(spread_out(fin1[:c2], LANES), 2 * LANES), ta...  1.55 us
    transpose x4, local copies, waits for them, and re-layouts, wide(): w = w.transpose(0, 3, 1, 2, 4).reshape(2, 3 * LANES, -1)  1.52 us

commit v1 on v0

--- a/solution.py
+++ b/solution.py
@@ -131,6 +131,84 @@
     return n, up_to(-(-length // n), 16)
 
 
+def prepare(levels, given, made, stage):
+    w0_in, w1_in, mid0, mid1, fin0, fin1 = given
+    w0, w1, wd0, wd1a, wd1v, wd2, wd2v = made
+    c0, c1, c2, c3 = (lv.chan for lv in levels)
+
+    def shifted(row, n, off, width, to):
+        k, s = divmod(off, LANES)
+        a = stage[row : row + n, k * LANES : (k + 1) * LANES]
+        ids = lax.broadcasted_iota(jnp.int32, a.shape, 1)
+        if s + width > LANES:
+            a = jnp.where(ids >= s, a, stage[row : row + n, (k + 1) * LANES : (k + 2) * LANES])
+        if (to - s) % LANES:
+            a = pltpu.roll(a, (to - s) % LANES, 1)
+        if width == LANES:
+            return a
+        return jnp.where((ids >= to) & (ids < to + width), a, 0.0)
+
+    def fill(value):
+        n, k = value.shape
+        stage[0:n, 0:k] = value.astype(F32)
+
+    for i in range(2):
+        fill(w0_in[i])
+        for q in range(3):
+            offs = [c0 * (3 * p + q) for p in range(3)]
+            cut = LANES - 2 * c0
+            tile = shifted(0, c0, offs[0], c0, 0) + shifted(0, c0, offs[1], c0, c0)
+            tile = tile + shifted(0, c0, offs[2], cut, 2 * c0)
+            w0[i, q * LANES : q * LANES + c0, 0:LANES] = tile.astype(BF16)
+            tile = shifted(0, c0, offs[2] + cut, c0 - cut, 0)
+            w0[i, q * LANES : q * LANES + c0, LANES : 2 * LANES] = tile.astype(BF16)
+        fill(w1_in[i])
+        for q in range(3):
+            for p in range(3):
+                tile = shifted(0, c1, c1 * (3 * p + q), c1, 0)
+                w1[i, q * LANES : q * LANES + c1, p * LANES : (p + 1) * LANES] = tile.astype(BF16)
+
+    def apart(value, to, row):
+        fill(value)
+        for t in range(9):
+            to[row : row + c1, t * LANES : (t + 1) * LANES] = shifted(0, c1, c1 * t, c1, 0).astype(BF16)
+
+    for k in range(c2 // c1):
+        apart(fin1[0, k * c1 : (k + 1) * c1, :], wd1a, k * c1)
+    apart(mid1[0, 0], wd1a, 2 * LANES)
+    for k in range(c3 // c1):
+        apart(fin1[0, c2 + k * c1 : c2 + (k + 1) * c1, :], wd2v, k * c1)
+
+    tall = up_to(9 * c0, LANES)
+
+    def turned():
+        return stage[0:LANES, 0:tall].T.astype(BF16)
+
+    stage[0:LANES, 0:tall] = jnp.zeros((LANES, tall), F32)
+    for k in range(2):
+        stage[k * c0 : (k + 1) * c0, 0 : 9 * c0] = mid0[0, k].astype(F32)
+    flat = turned()
+    for t in range(9):
+        wd0[t * LANES : t * LANES + c0, LANES : 2 * LANES] = flat[t * c0 : (t + 1) * c0, :]
+        wd0[t * LANES : t * LANES + c0, 0:LANES] = fin0[t * c0 : (t + 1) * c0, 0:LANES]
+    stage[0:LANES, 0:tall] = jnp.zeros((LANES, tall), F32)
+    stage[c2 - LANES : c2 - LANES + c0, 0 : 9 * c0] = mid0[0, 2].astype(F32)
+    flat = turned()
+    for t in range(9):
+        wd1v[t * LANES + c0 : t * LANES + 2 * c0, LANES : 2 * LANES] = flat[t * c0 : (t + 1) * c0, :]
+    fill(fin0[...])
+    depth = wd2.shape[0] // 9
+    for t in range(9):
+        wd1v[t * LANES : t * LANES + c0, 0:LANES] = shifted(t * c0, c0, c1, LANES, 0).astype(BF16)
+        tile = shifted(t * c0, c0, c1 + LANES, c2 - LANES, 0)
+        wd1v[t * LANES : t * LANES + c0, LANES : 2 * LANES] = tile.astype(BF16)
+        row = t * depth + c2
+        wd2[row : row + depth - c2, :] = jnp.zeros((depth - c2, c3), BF16)
+        for j in range(c3 // LANES):
+            tile = shifted(t * c0, c0, c1 + c2 + j * LANES, LANES, 0)
+            wd2[row : row + c0, j * LANES : (j + 1) * LANES] = tile.astype(BF16)
+
+
 def body(levels, *refs):
     refs = list(refs)
 
@@ -140,22 +218,33 @@
         return out
 
     feats, halos = take(4), take(32)
-    w0, w1, w2_hbm, w3_hbm = take(4)
+    w0_in, w1_in, w2_hbm, w3_hbm = take(4)
     biases = take(4)
-    up1, up2, up3, wd0, wd1a, wd1v, wd2_hbm = take(7)
+    up1, up2, up3, mid0, mid1, fin0, fin1, fin2_hbm = take(8)
     outs = take(4)
     xs, hs = take(4), take(4)
     spread, odd, cols2, cols3 = take(4)
-    w2, w3, wd2 = take(3)
+    w2, w3 = take(2)
+    w0, w1, wd0, wd1a, wd1v, wd2, wd2v, stage, bpad = take(9)
     t01, v0, t2, v1, u0, u1, u2 = take(7)
     (sems,) = take(1)
     l0, l1, l2, l3 = levels
-    copies = [
-        pltpu.make_async_copy(a, b, sems.at[i])
-        for i, (a, b) in enumerate(((w2_hbm, w2), (w3_hbm, w3), (wd2_hbm, wd2)))
+    copies = [pltpu.make_async_copy(a, b, sems.at[i]) for i, (a, b) in enumerate(((w2_hbm, w2), (w3_hbm, w3)))]
+    depth = wd2.shape[0] // 9
+    for ref in (w0, w1, wd0, wd1a, wd1v, bpad):
+        ref[...] = jnp.zeros_like(ref)
+    fin2_copies = [
+        pltpu.make_async_copy(
+            fin2_hbm.at[pl.ds(t * l2.chan, l2.chan)], wd2.at[pl.ds(t * depth, l2.chan)], sems.at[2 + t]
+        )
+        for t in range(9)
     ]
-    for c in copies:
+    for c in copies + fin2_copies:
         c.start()
+
+    prepare(levels, (w0_in, w1_in, mid0, mid1, fin0, fin1), (w0, w1, wd0, wd1a, wd1v, wd2, wd2v), stage)
+    for l in (0, 1):
+        bpad[l, 0:2, 0 : levels[l].chan] = biases[l][...]
 
     ty, tx = lax.axis_index("ty"), lax.axis_index("tx")
     top, bottom = ty == 0, ty == lax.axis_size("ty") - 1
@@ -278,7 +367,7 @@
             else:
                 cols2[0:m, k + 128 : k + 256] = (tile + piece(odd, 0, t + 1)).astype(BF16)
                 cols2[0:m, k + 256 : k + 384] = piece(odd, 1, t + 1).astype(BF16)
-        y = lax.dot_general(cols2[0:m, :], weight, NT, preferred_element_type=F32) + bias[:, 0 : lv.chan]
+        y = lax.dot_general(cols2[0:m, :], weight, NT, preferred_element_type=F32) + bias
         for p in range(2):
             w = min(LANES, lv.chan - p * LANES)
             part = y[:, p * LANES : p * LANES + w]
@@ -303,9 +392,9 @@
 
     for l in (0, 1):
         lv = levels[l]
-        wide_conv(l, xs[l], hs[l], (w0, w1)[l].at[0], biases[l][0:1, :], lv.first(), False)
+        wide_conv(l, xs[l], hs[l], (w0, w1)[l].at[0], bpad[l, 0:1, :], lv.first(), False)
         blank(hs[l], lv, lv.rim + 1, 1)
-        wide_conv(l, hs[l], xs[l], (w0, w1)[l].at[1], biases[l][1:2, :], lv.second(), True)
+        wide_conv(l, hs[l], xs[l], (w0, w1)[l].at[1], bpad[l, 1:2, :], lv.second(), True)
         blank(xs[l], lv, lv.rim, 0)
 
     hs[2][1, :, :] = jnp.zeros((l2.total, LANES), F32)
@@ -333,7 +422,7 @@
             jnp.concatenate([gathered(xs[0], 0, l0, l1, i0 + r, t) for r in range(4)], axis=0).astype(BF16)
             for t in range(9)
         ]
-        o = lax.dot_general(jnp.concatenate(taps, axis=1), wd0[...], NT, preferred_element_type=F32)
+        o = lax.dot_general(jnp.concatenate(taps, axis=1), wd0[...], NN, preferred_element_type=F32)
         at = pl.multiple_of((i0 + l1.lead) * l1.pitch - l1.tail, 8)
         t01[0, pl.ds(at, 4 * l1.pitch), :] = o[:, 0:LANES]
         v0[0, pl.ds(at, 4 * l1.pitch), :] = jnp.maximum(o[:, LANES:], 0.0)
@@ -345,15 +434,15 @@
     at = l2.at(-2) - l2.tail
     span = rows * l2.pitch
 
-    def down1(src, weight):
+    def down1(src, weight, form):
         taps = [
             jnp.concatenate([gathered(src, 0, l1, l2, i, t) for i in range(-2, l2.rows)], axis=0).astype(BF16)
             for t in range(9)
         ]
-        return lax.dot_general(jnp.concatenate(taps, axis=1), weight[...], NT, preferred_element_type=F32)
-
-    o = down1(xs[1], wd1a)
-    e = down1(v0, wd1v)
+        return lax.dot_general(jnp.concatenate(taps, axis=1), weight[...], form, preferred_element_type=F32)
+
+    o = down1(xs[1], wd1a, NT)
+    e = down1(v0, wd1v, NN)
     second = o[:, LANES : 2 * LANES] + e[:, LANES : 2 * LANES]
     ids = lane(second.shape)
     t2[0, 0:span, :] = o[:, 0:LANES] + e[:, 0:LANES]
@@ -361,18 +450,21 @@
     v1[0, pl.ds(at, span), :] = jnp.where(ids >= 64, jnp.maximum(second, 0.0), 0.0)
     v1[1, pl.ds(at, span), :] = jnp.maximum(o[:, 2 * LANES :], 0.0)
     blank(v1, l2, 1, 0)
-    taps = []
-    for t in range(9):
-        for p in range(3):
-            parts = []
-            for i in range(l3.rows):
-                piece = gathered(xs[2] if p < 2 else v1, p if p < 2 else 1, l2, l3, i, t, l3.cols)
-                if p == 1:
-                    piece = piece + gathered(v1, 0, l2, l3, i, t, l3.cols)
-                parts.append(piece)
-            taps.append(jnp.concatenate(parts, axis=0).astype(BF16))
-    copies[2].wait()
-    t3 = lax.dot_general(jnp.concatenate(taps, axis=1), wd2[...], NN, preferred_element_type=F32)
+    def tap3(p, t):
+        parts = []
+        for i in range(l3.rows):
+            piece = gathered(xs[2] if p < 2 else v1, p if p < 2 else 1, l2, l3, i, t, l3.cols)
+            if p == 1:
+                piece = piece + gathered(v1, 0, l2, l3, i, t, l3.cols)
+            parts.append(piece)
+        return jnp.concatenate(parts, axis=0).astype(BF16)
+
+    taps = jnp.concatenate([tap3(2, t) for t in range(9)], axis=1)
+    t3 = lax.dot_general(taps, wd2v[...], NT, preferred_element_type=F32)
+    taps = jnp.concatenate([tap3(p, t) for t in range(9) for p in range(2)], axis=1)
+    for c in fin2_copies:
+        c.wait()
+    t3 = t3 + lax.dot_general(taps, wd2[...], NN, preferred_element_type=F32)
 
     def center(l, i):
         lv = levels[l]
@@ -386,9 +478,9 @@
 
     c0, c1, c2 = l0.chan, l1.chan, l2.chan
     a3 = a3.astype(BF16)
-    up3_0 = lax.dot_general(a3, up3[0:c0, :], NT, preferred_element_type=F32)
-    up3_1 = lax.dot_general(a3, up3[c0 : c0 + c1, :], NT, preferred_element_type=F32)
-    up3_2 = lax.dot_general(a3, up3[c0 + c1 :, :], NT, preferred_element_type=F32)
+    up3_0 = lax.dot_general(a3, up3[0, 0:c0, :], NT, preferred_element_type=F32)
+    up3_1 = lax.dot_general(a3, up3[0, c0 : c0 + c1, :], NT, preferred_element_type=F32)
+    up3_2 = lax.dot_general(a3, up3[0, c0 + c1 :, :], NT, preferred_element_type=F32)
 
     def enlarge(value, dst, plane, width, rows, cols):
         for i in range(rows):
@@ -404,8 +496,8 @@
     enlarge(up3_2[:, LANES:], u2, 3, c2 - LANES, l3.rows, l3.cols)
     a2 = jnp.concatenate([center(2, i) for i in range(l2.rows)], axis=0)
     a2b = a2.astype(BF16)
-    up2_0 = lax.dot_general(a2b, up2[0:c0, :], NT, preferred_element_type=F32) + u2[0, :, 0:c0]
-    up2_1 = lax.dot_general(a2b, up2[c0:, :], NT, preferred_element_type=F32) + u2[1, :, 0:c1]
+    up2_0 = lax.dot_general(a2b, up2[0, 0:c0, :], NT, preferred_element_type=F32) + u2[0, :, 0:c0]
+    up2_1 = lax.dot_general(a2b, up2[0, c0:, :], NT, preferred_element_type=F32) + u2[1, :, 0:c1]
     for i in range(l2.rows):
         for p in range(2):
             w = min(LANES, c2 - p * LANES)
@@ -428,7 +520,7 @@
             outs[1][i, :, :] = jnp.maximum(total, 0.0).astype(BF16)
         a1 = jnp.concatenate(lines, axis=0).astype(BF16)
         n = 4 * l1.cols
-        y = lax.dot_general(a1, up1[...], NT, preferred_element_type=F32)
+        y = lax.dot_general(a1, up1[0], NT, preferred_element_type=F32)
         y = y + u1[0, pl.ds(pl.multiple_of(k * n, 8), n), 0:c0]
         for r in range(4):
             line = y[r * l1.cols : (r + 1) * l1.cols, :]
@@ -444,16 +536,6 @@
     rows_loop(l1.rows // 4, join1)
 
 
-def spread_out(w, lanes):
-    n = w.shape[0]
-    w = w.reshape(n, 9, -1)
-    return jnp.pad(w, ((0, 0), (0, 0), (0, lanes - w.shape[2])))
-
-
-def tall(w, n):
-    return jnp.pad(w, ((0, n - w.shape[0]),) + ((0, 0),) * (w.ndim - 1))
-
-
 def per_device(*args):
     feats, weights, biases, rest = args[0:4], args[4:8], args[8:12], args[12:20]
     feats = [f.transpose(1, 2, 0) for f in feats]
@@ -461,42 +543,8 @@
     l0, l1, l2, l3 = levels
     c0, c1, c2, c3 = (lv.chan for lv in levels)
     halos = halos_of(levels, feats)
-    up1, up2, up3, mid0, mid1, fin0, fin1, fin2 = (r[0] for r in rest)
-
-    def wide(w, c, deep):
-        w = w.reshape(2, c, 3, 3, c)
-        if 3 * c > 2 * LANES:
-            w = jnp.pad(w, ((0, 0),) * 4 + ((0, LANES - c),))
-        w = jnp.pad(w, ((0, 0), (0, LANES - c)) + ((0, 0),) * 3)
-        w = w.transpose(0, 3, 1, 2, 4).reshape(2, 3 * LANES, -1)
-        return jnp.pad(w, ((0, 0), (0, 0), (0, deep - w.shape[2])))
-
-    w0 = wide(weights[0], c0, 2 * LANES)
-    w1 = wide(weights[1], c1, 3 * LANES)
-    bs = [jnp.pad(b, ((0, 0), (0, up_to(b.shape[1], LANES) - b.shape[1]))) for b in biases]
-    wd0 = jnp.concatenate(
-        [
-            tall(spread_out(fin0[:c1], LANES), LANES),
-            tall(spread_out(mid0[0:2].reshape(2 * c0, -1), LANES), LANES),
-        ]
-    ).reshape(2 * LANES, -1)
-    wd1a = jnp.concatenate(
-        [tall(spread_out(fin1[:c2], LANES), 2 * LANES), tall(spread_out(mid1[0], LANES), LANES)]
-    ).reshape(3 * LANES, -1)
-    late = jnp.pad(spread_out(mid0[2], c0), ((0, 0), (0, 0), (c0, 0)))
-    wd1v = tall(
-        jnp.concatenate([spread_out(fin0[c1 : c1 + c2], 2 * c0), late]), 2 * LANES
-    )
-    wd1v = jnp.pad(wd1v, ((0, 0), (0, 0), (0, LANES - 2 * c0))).reshape(2 * LANES, -1)
-
-    def deep(w, pad):
-        w = w.T.reshape(9, -1, c3)
-        return jnp.pad(w, ((0, 0), (0, pad - w.shape[1]), (0, 0)))
-
-    wd2 = jnp.concatenate(
-        [deep(fin2, c2), deep(fin0[c1 + c2 :], 64), deep(fin1[c2:], LANES)], axis=1
-    ).reshape(-1, c3)
-
+    up1, up2, up3, mid0, mid1, fin0, fin1, fin2 = rest
+    fin0, fin2 = fin0[0].T, fin2[0].T
     vmem, any_ = pl.BlockSpec(memory_space=pltpu.VMEM), pl.BlockSpec(memory_space=pl.ANY)
     V = pltpu.VMEM
     maps = [V((lv.planes, lv.total, LANES), F32) for lv in levels]
@@ -509,7 +557,15 @@
         V((m3, 9 * c3), BF16),
         V(weights[2].shape, BF16),
         V(weights[3].shape, BF16),
-        V(wd2.shape, BF16),
+        V((2, 3 * LANES, 2 * LANES), BF16),
+        V((2, 3 * LANES, 3 * LANES), BF16),
+        V((9 * LANES, 2 * LANES), BF16),
+        V((3 * LANES, 9 * LANES), BF16),
+        V((9 * LANES, 2 * LANES), BF16),
+        V((9 * up_to(c2, LANES), c3), BF16),
+        V((c3, 9 * LANES), BF16),
+        V((up_to(9 * c0, 8), up_to(max(9 * c1, fin0.shape[1]), LANES) + LANES), F32),
+        V((2, 8, LANES), F32),
         V((1, l1.total, LANES), F32),
         V((1, l1.total, LANES), F32),
         V((2, (l2.rows + 2) * l2.pitch, LANES), F32),
@@ -517,16 +573,16 @@
         V((1, l0.cols, LANES), F32),
         V((2, l1.rows * l1.cols, LANES), F32),
         V((4, l2.rows * l2.cols, LANES), F32),
-        pltpu.SemaphoreType.DMA((3,)),
+        pltpu.SemaphoreType.DMA((11,)),
     ]
     outs = pl.pallas_call(
         functools.partial(body, levels),
         out_shape=[jax.ShapeDtypeStruct(f.shape, BF16) for f in feats],
-        in_specs=[vmem] * 36 + [vmem] * 2 + [any_] * 2 + [vmem] * 4 + [vmem] * 6 + [any_],
+        in_specs=[vmem] * 38 + [any_] * 2 + [vmem] * 11 + [any_],
         out_specs=[vmem] * 4,
         scratch_shapes=scratch,
         compiler_params=pltpu.CompilerParams(vmem_limit_bytes=60 * 2**20),
-    )(*feats, *halos, w0, w1, weights[2], weights[3], *bs, up1, up2, up3, wd0, wd1a, wd1v, wd2)
+    )(*feats, *halos, *weights, *biases, up1, up2, up3, mid0, mid1, fin0, fin1, fin2)
     return tuple(o.transpose(2, 0, 1) for o in outs)
 
 

time: 72.9 us -> 52.4 us (0.72)
  local copies, waits for them, and re-layouts: 23.8 us -> 5.57 us
  other arithmetic: 3.09 us -> 0 us
  Pallas kernels: 44.9 us -> 46 us
    reshape x7 -> x0, local copies, waits for them, and re-layouts: 5.51 us -> none  [the longest x3 1.62 us: wide(): w = w.transpose(0, 3, 1, 2, 4).reshape(2, 3 * LANES, -1)]
    pad x5 -> x0, local copies, waits for them, and re-layouts: 4.69 us -> none  [the longest x3 3.79 us: per_device(): jnp.pad(b, ((0, 0), (0, up_to(b.shape[1], LANES) - b.shape[1])))]
    slice x11 -> x0, local copies, waits for them, and re-layouts: 4.25 us -> none  [the longest x1 1.21 us: per_device(): fin0[c1 + c2:]]
    concatenate x4 -> x0, other arithmetic: 3.09 us -> none  [the longest x1 2.77 us: per_device(): jnp.concatenate([deep(fin2, c2), deep(fin0[c1 + c2:], 64), deep(fin1[c2:]...]
    unnamed x13 -> x2, local copies, waits for them, and re-layouts: 7.66 us -> 5.57 us
    transpose x4 -> x0, local copies, waits for them, and re-layouts: 1.52 us -> none  [wide(): w = w.transpose(0, 3, 1, 2, 4).reshape(2, 3 * LANES, -1)]
    pallas_call x1, Pallas kernels: 29.7 us -> 30.8 us  [per_device(): pl.pallas_call(functools.partial(body, levels), out_shape=[jax.ShapeDtype...]
where the time goes in v1:
time: 52.4 us; the launch traced here: 52.3 us
  Pallas kernels  46 us (88%)
  local copies, waits for them, and re-layouts  5.57 us (11%)
  between operations  0.65 us (1%)
    pallas_call x1, Pallas kernels, per_device(): pl.pallas_call(functools.partial(body, levels), out_shape=[jax.ShapeDtype...  30.8 us
    pallas_call x1, Pallas kernels, halos_of(): pl.pallas_call(functools.partial(exchange, levels), out_shape=shapes, in_...  15.2 us
    unnamed x2, local copies, waits for them, and re-layouts  5.57 us

profile of v1, /device:TPU:22, one launch (start us, length us, event | category | flops | bytes accessed | tf_op | source)
XLA Modules:
  0.0 52.3 jit_solution(12906381480888760284)
XLA Ops:
  0.6 2.7 %copy.24 = bf16[48,64,64]{0,2,1:T(8,128)(2,1)} copy(bf16[48,64,64]{2,1,0:T(8,128)(2,1)} %param.20) | data formatting | bytes 786432 | tf_op args[0]
  3.3 15.2 %shard_map.219 = (bf16[2,8,48]{2,1,0:T(8,128)(2,1)}, bf16[2,64,48]{2,1,0:T(8,128)(2,1)}, bf16[2,16,48]{2,1,0:T(8,128)(2,1)}, bf16[64,8,48]{2,1,0:T(8,128)(2,1)},...) custom-call(bf16[64,64,48]{2,1,0:T(8,128)(2,1)} %bitcast.14, ...), custom_call_target="tpu_custom_call" | custom-call | tf_op jit(solution)/shard_map/pallas_call | solution.py:119
  18.5 30.8 %shard_map.220 = (bf16[64,64,48]{2,1,0:T(8,128)(2,1)}, bf16[32,32,96]{2,1,0:T(8,128)(2,1)}, bf16[16,16,192]{2,1,0:T(8,128)(2,1)}, bf16[8,8,384]{2,1,0:T(8,128)(2,1)}) custom-call(bf16[64,64,48]{2,1,0:T(8,128)(2,1)} %bitcast.15, bf16[32,32,96]{2,1,0:T(8,128)(2,1)} %bitcast.19, bf16[16,16,192]{2,1,0:T(8,128)(2,1)} %bitcast.22, bf16[8,8,384]{2,1,0:T(8,128)(2,1)} %bitcast.24, ...), custom_call_target="tpu_custom_call" | custom-call | tf_op jit(solution)/shard_map/pallas_call | solution.py:578
  49.4 2.9 %copy.25 = bf16[48,64,64]{2,1,0:T(8,128)(2,1)} copy(bf16[48,64,64]{0,2,1:T(8,128)(2,1)} %bitcast.17) | data formatting | bytes 786432

commit v2 on v1

--- a/solution.py
+++ b/solution.py
@@ -30,6 +30,9 @@
         self.planes = up_to(self.chan, LANES) // LANES
         self.near = up_to(self.low, 8)
         self.total = (self.lead + self.rows + 4) * self.pitch
+        self.folds = 2 if 2 * self.chan <= LANES else 1
+        self.lines = self.rows // self.folds
+        self.wide = LANES if self.folds == 2 else self.chan
 
     def at(self, row, col=0):
         return (row + self.lead) * self.pitch + col
@@ -43,11 +46,19 @@
         return start, self.at(self.rows - 1) + self.cols - start
 
 
-def source_of(lv, way):
+def window(lv, way):
+    lines = lv.lines
+    if way[0] == 0:
+        return 0, lines
+    return (lines - lv.near, lv.near) if way[0] > 0 else (0, 8)
+
+
+def message(lv, way):
     dy, dx = way
-    rows = (0, lv.rows) if dy == 0 else ((lv.rows - lv.low, lv.low) if dy > 0 else (0, 2))
-    cols = (0, lv.cols) if dx == 0 else ((lv.cols - lv.near, lv.near) if dx > 0 else (0, 8))
-    return rows, cols
+    if dx == 0:
+        rows = lv.low if dy > 0 else 2
+        return (rows, lv.cols // lv.folds, lv.wide)
+    return (lv.low if dx > 0 else 2, window(lv, way)[1], lv.wide)
 
 
 def on_map(way, side):
@@ -60,9 +71,12 @@
 
 
 def exchange(levels, *refs):
-    feats, outs, (send, recv) = refs[:4], refs[4:36], refs[36:]
+    feats, outs, turned = refs[:4], refs[4:36], refs[36]
+    rows_sent, cols_sent = refs[37:39], refs[39:47]
+    stage, maps, side, send, recv = refs[47:]
     here = {a: lax.axis_index(a) for a in ("ty", "tx")}
     barrier = pltpu.get_barrier_semaphore()
+    l0 = levels[0]
 
     def there(way):
         return {"ty": here["ty"] + way[0], "tx": here["tx"] + way[1]}
@@ -76,17 +90,68 @@
             pl.semaphore_signal(barrier, 1, device_id=there(way))
 
         count = count + jnp.where(ok, 1, 0)
+
+    C, R, W = l0.chan, l0.rows, l0.cols
+
+    def load(i, _):
+        stage[pl.ds(pl.multiple_of(i * R, 8), R), :] = feats[0][i].astype(F32)
+        return 0
+
+    lax.fori_loop(0, C, load, 0)
+
+    def turn(r, _):
+        value = stage[pl.ds(r, C, stride=R), :].T
+        maps[pl.ds(pl.multiple_of(r * W, 8), W), 0:C] = value
+        turned[r] = value.astype(BF16)
+        return 0
+
+    lax.fori_loop(0, R, turn, 0)
+
+    def folded(a, b):
+        ids = lax.broadcasted_iota(jnp.int32, a.shape, 1)
+        a, b = jnp.where(ids < C, a, 0.0), jnp.where(ids < C, b, 0.0)
+        return (a + pltpu.roll(b, LANES // 2, 1)).astype(BF16)
+
+    half = W // 2
+    for to, first, n in ((rows_sent[0], R - l0.low, l0.low), (rows_sent[1], 0, 2)):
+        for i in range(n):
+            at = (first + i) * W
+            to[i] = folded(maps[at : at + half, :], maps[at + half : at + W, :])
+    half = R // 2
+    for to, first, n in ((cols_sent[0], W - l0.low, l0.low), (cols_sent[1], 0, 2)):
+        for i in range(n):
+            a = maps[pl.ds(first + i, half, stride=W), :]
+            to[i] = folded(a, maps[pl.ds(half * W + first + i, half, stride=W), :])
+    for l in range(1, 4):
+        lv = levels[l]
+        for d, (base, n) in enumerate(((lv.cols - 8, lv.low), (0, 2))):
+            to = cols_sent[2 * l + d]
+            size = lv.rows * 8
+            for p in range(lv.planes):
+                w = min(LANES, lv.chan - p * LANES)
+                block = feats[l][:, base : base + 8, p * LANES : p * LANES + w].astype(F32)
+                side[6 * l + 3 * d + p, 0:size, 0:w] = block.reshape(size, w)
+                for i in range(n):
+                    at = i + (8 - n if d == 0 else 0)
+                    value = side[6 * l + 3 * d + p, pl.ds(at, lv.rows, stride=8), 0:w]
+                    to[i, :, p * LANES : p * LANES + w] = value.astype(BF16)
+
     pl.semaphore_wait(barrier, count)
 
     def copy(l, k):
-        way = WAYS[k]
-        (r, nr), (c, nc) = source_of(levels[l], way)
+        lv, way = levels[l], WAYS[k]
+        dy, dx = way
+        if dx:
+            src = cols_sent[2 * l + (0 if dx > 0 else 1)]
+            first, n = window(lv, way)
+            if dy:
+                src = src.at[:, pl.ds(first, n)]
+        elif l == 0:
+            src = rows_sent[0 if dy > 0 else 1]
+        else:
+            src = feats[l].at[pl.ds(lv.rows - lv.low, lv.low) if dy > 0 else pl.ds(0, 2)]
         return pltpu.make_async_remote_copy(
-            feats[l].at[pl.ds(r, nr), pl.ds(c, nc)],
-            outs[8 * l + k],
-            send.at[8 * l + k],
-            recv.at[8 * l + k],
-            device_id=there(way),
+            src, outs[8 * l + k], send.at[8 * l + k], recv.at[8 * l + k], device_id=there(way)
         )
 
     for k, way in enumerate(WAYS):
@@ -110,18 +175,26 @@
 
 
 def halos_of(levels, feats):
-    shapes = []
-    for lv in levels:
-        for way in WAYS:
-            (_, nr), (_, nc) = source_of(lv, way)
-            shapes.append(jax.ShapeDtypeStruct((nr, nc, lv.chan), BF16))
-    hbm = pl.BlockSpec(memory_space=pl.ANY)
+    V = pltpu.VMEM
+    l0 = levels[0]
+    shapes = [jax.ShapeDtypeStruct(message(lv, way), BF16) for lv in levels for way in WAYS]
+    shapes.append(jax.ShapeDtypeStruct((l0.rows, l0.cols, l0.chan), BF16))
+    vmem, hbm = pl.BlockSpec(memory_space=pltpu.VMEM), pl.BlockSpec(memory_space=pl.ANY)
+    scratch = [V(message(l0, (d, 0)), BF16) for d in (1, -1)]
+    scratch += [V(message(lv, (0, d)), BF16) for lv in levels for d in (1, -1)]
+    scratch += [
+        V((l0.chan * l0.rows, l0.cols), F32),
+        V((l0.rows * l0.cols, LANES), F32),
+        V((24, 8 * levels[1].rows, LANES), F32),
+        pltpu.SemaphoreType.DMA((32,)),
+        pltpu.SemaphoreType.DMA((32,)),
+    ]
     return pl.pallas_call(
         functools.partial(exchange, levels),
         out_shape=shapes,
-        in_specs=[hbm] * 4,
-        out_specs=[hbm] * 32,
-        scratch_shapes=[pltpu.SemaphoreType.DMA((32,))] * 2,
+        in_specs=[vmem] * 4,
+        out_specs=[hbm] * 32 + [vmem],
+        scratch_shapes=scratch,
         compiler_params=pltpu.CompilerParams(collective_id=0, has_side_effects=True),
     )(*feats)
 
@@ -272,22 +345,55 @@
         ref[...] = jnp.zeros_like(ref)
     for l, lv in enumerate(levels):
 
-        def place(source, row, col, l=l, lv=lv, skip=0, keep=None):
+        def place(source, row, l=l, lv=lv):
             def run(i):
-                at = pl.multiple_of((i + row + lv.lead) * lv.pitch + col, 8)
-                put(l, at + skip, source[i].astype(F32)[skip:keep])
+                at = pl.multiple_of((i + row + lv.lead) * lv.pitch, 8)
+                put(l, at, source[i].astype(F32))
 
             rows_loop(source.shape[0], run)
 
-        place(feats[l], 0, 0)
+        def place_rows(source, row, l=l, lv=lv):
+            if lv.folds == 1:
+                return place(source, row)
+            half = lv.cols // 2
+            for i in range(source.shape[0]):
+                value = source[i].astype(F32)
+                put(l, lv.at(row + i), value[:, : lv.chan])
+                put(l, lv.at(row + i, half), pltpu.roll(value, LANES // 2, 1)[:, : lv.chan])
+
+        def place_cols(source, way, l=l, lv=lv):
+            dy, dx = way
+            for i in range(source.shape[0]):
+                col = i - lv.low if dx > 0 else lv.cols + i
+                value = source[i].astype(F32)
+                both = [value]
+                if lv.folds == 2:
+                    both = [value, pltpu.roll(value, LANES // 2, 1)]
+                if dy > 0:
+                    pieces = [(-lv.low, both[-1][lv.near - lv.low :])]
+                elif dy < 0:
+                    pieces = [(lv.rows, both[0][:2])]
+                else:
+                    pieces = [(j * lv.lines, v) for j, v in enumerate(both)]
+                for row, v in pieces:
+                    for p in range(lv.planes):
+                        w = min(LANES, lv.chan - p * LANES)
+                        at = pl.ds(lv.at(row, col), v.shape[0], stride=lv.pitch)
+                        part = v[:, p * LANES : p * LANES + w]
+                        if w < LANES:
+                            part = jnp.concatenate([part, jnp.zeros((v.shape[0], LANES - w), F32)], axis=1)
+                        xs[l][p, at, :] = part
+
+        place(feats[l], 0)
         for k, way in enumerate(WAYS):
-            dy, dx = way
-            row = {0: 0, 1: -lv.low, -1: lv.rows}[dy]
-            col, skip, keep = {0: (0, 0, None), 1: (-lv.near, lv.near - lv.low, None), -1: (lv.cols, 0, 2)}[dx]
 
             @pl.when(on_map(way, -1))
-            def _(k=k, row=row, col=col, skip=skip, keep=keep):
-                place(halos[8 * l + k], row, col, skip=skip, keep=keep)
+            def _(k=k, way=way):
+                source = halos[8 * l + k]
+                if way[1]:
+                    place_cols(source, way)
+                else:
+                    place_rows(source, -lv.low if way[0] > 0 else lv.rows)
 
     def blank(ref, lv, low, high):
         planes = ref.shape[0]
@@ -538,11 +644,12 @@
 
 def per_device(*args):
     feats, weights, biases, rest = args[0:4], args[4:8], args[8:12], args[12:20]
-    feats = [f.transpose(1, 2, 0) for f in feats]
-    levels = [Level(l, f.shape) for l, f in enumerate(feats)]
+    levels = [Level(l, f.shape[1:] + f.shape[:1]) for l, f in enumerate(feats)]
+    feats = [feats[0]] + [f.transpose(1, 2, 0) for f in feats[1:]]
     l0, l1, l2, l3 = levels
     c0, c1, c2, c3 = (lv.chan for lv in levels)
-    halos = halos_of(levels, feats)
+    *halos, first = halos_of(levels, feats)
+    feats[0] = first
     up1, up2, up3, mid0, mid1, fin0, fin1, fin2 = rest
     fin0, fin2 = fin0[0].T, fin2[0].T
     vmem, any_ = pl.BlockSpec(memory_space=pltpu.VMEM), pl.BlockSpec(memory_space=pl.ANY)

time: 52.4 us -> 50.2 us (0.958)
  local copies, waits for them, and re-layouts: 5.57 us -> 2.9 us
    unnamed x2 -> x1, local copies, waits for them, and re-layouts: 5.57 us -> 2.9 us
    pallas_call x1, Pallas kernels: 15.2 us -> 17 us  [halos_of(): pl.pallas_call(functools.partial(exchange, levels), out_shape=shapes, in_...]
    pallas_call x1, Pallas kernels: 30.8 us -> 29.5 us  [per_device(): pl.pallas_call(functools.partial(body, levels), out_shape=[jax.ShapeDtype...]
where the time goes in v2:
time: 50.2 us; the launch traced here: 50.1 us
  Pallas kernels  46.5 us (93%)
  local copies, waits for them, and re-layouts  2.9 us (6%)
  between operations  0.65 us (1%)
    pallas_call x1, Pallas kernels, per_device(): pl.pallas_call(functools.partial(body, levels), out_shape=[jax.ShapeDtype...  29.5 us
    pallas_call x1, Pallas kernels, halos_of(): pl.pallas_call(functools.partial(exchange, levels), out_shape=shapes, in_...  17 us
    unnamed x1, local copies, waits for them, and re-layouts  2.9 us

profile of v2, /device:TPU:22, one launch (start us, length us, event | category | flops | bytes accessed | tf_op | source)
XLA Modules:
  0.0 50.1 jit_solution(10274547509829587142)
XLA Ops:
  0.6 17.0 %shard_map.219 = (bf16[2,8,128]{2,1,0:T(8,128)(2,1)}, bf16[2,32,128]{2,1,0:T(8,128)(2,1)}, bf16[9,8,128]{2,1,0:T(8,128)(2,1)}, bf16[2,32,128]{2,1,0:T(8,128)(2,1...) custom-call(bf16[48,64,64]{2,1,0:T(8,128)(2,1)} %refs_0_.1, ...), custom_call_target="tpu_custom_call" | custom-call | tf_op jit(solution)/shard_map/pallas_call | solution.py:192
  17.7 29.5 %shard_map.220 = (bf16[64,64,48]{2,1,0:T(8,128)(2,1)}, bf16[32,32,96]{2,1,0:T(8,128)(2,1)}, bf16[16,16,192]{2,1,0:T(8,128)(2,1)}, bf16[8,8,384]{2,1,0:T(8,128)(2,1)}) custom-call(bf16[64,64,48]{2,1,0:T(8,128)(2,1)} %get-tuple-element.41.refs_0_, bf16[32,32,96]{2,1,0:T(8,128)(2,1)} %bitcast.15, bf16[16,16,192]{2,1,0:T(8,128)(2,1)} %bitcast.19, ...), custom_call_target="tpu_custom_call" | custom-call | tf_op jit(solution)/shard_map/pallas_call | solution.py:685
  47.2 2.9 %copy.24 = bf16[48,64,64]{2,1,0:T(8,128)(2,1)} copy(bf16[48,64,64]{0,2,1:T(8,128)(2,1)} %bitcast.16) | data formatting | bytes 786432

commit v3 on v2

--- a/solution.py
+++ b/solution.py
@@ -8,6 +8,7 @@
 from jax.sharding import PartitionSpec as P
 
 RIMS = (7, 3, 1, 0)
+GROUP = 3
 LANES = 128
 NT = (((1,), (1,)), ((), ()))
 NN = (((1,), (0,)), ((), ()))
@@ -93,19 +94,26 @@
 
     C, R, W = l0.chan, l0.rows, l0.cols
 
+    tall, wide = R + 1, W + 1
+
     def load(i, _):
-        stage[pl.ds(pl.multiple_of(i * R, 8), R), :] = feats[0][i].astype(F32)
+        for j in range(8):
+            at = pl.multiple_of(i * 8 * tall, 8) + j * tall
+            stage[pl.ds(at, R), :] = feats[0][8 * i + j].astype(F32)
         return 0
 
-    lax.fori_loop(0, C, load, 0)
-
-    def turn(r, _):
-        value = stage[pl.ds(r, C, stride=R), :].T
-        maps[pl.ds(pl.multiple_of(r * W, 8), W), 0:C] = value
-        turned[r] = value.astype(BF16)
+    lax.fori_loop(0, C // 8, load, 0)
+
+    def turn(i, _):
+        for j in range(8):
+            r = 8 * i + j
+            value = stage[pl.ds(r, C, stride=tall), :].T
+            at = pl.multiple_of(i * 8 * wide, 8) + j * wide
+            maps[pl.ds(at, W), 0:C] = value
+            turned[r] = value.astype(BF16)
         return 0
 
-    lax.fori_loop(0, R, turn, 0)
+    lax.fori_loop(0, R // 8, turn, 0)
 
     def folded(a, b):
         ids = lax.broadcasted_iota(jnp.int32, a.shape, 1)
@@ -115,25 +123,26 @@
     half = W // 2
     for to, first, n in ((rows_sent[0], R - l0.low, l0.low), (rows_sent[1], 0, 2)):
         for i in range(n):
-            at = (first + i) * W
+            at = (first + i) * wide
             to[i] = folded(maps[at : at + half, :], maps[at + half : at + W, :])
     half = R // 2
     for to, first, n in ((cols_sent[0], W - l0.low, l0.low), (cols_sent[1], 0, 2)):
         for i in range(n):
-            a = maps[pl.ds(first + i, half, stride=W), :]
-            to[i] = folded(a, maps[pl.ds(half * W + first + i, half, stride=W), :])
+            a = maps[pl.ds(first + i, half, stride=wide), :]
+            to[i] = folded(a, maps[pl.ds(half * wide + first + i, half, stride=wide), :])
     for l in range(1, 4):
         lv = levels[l]
         for d, (base, n) in enumerate(((lv.cols - 8, lv.low), (0, 2))):
             to = cols_sent[2 * l + d]
-            size = lv.rows * 8
             for p in range(lv.planes):
                 w = min(LANES, lv.chan - p * LANES)
-                block = feats[l][:, base : base + 8, p * LANES : p * LANES + w].astype(F32)
-                side[6 * l + 3 * d + p, 0:size, 0:w] = block.reshape(size, w)
+                slot = 6 * l + 3 * d + p
+                for r in range(lv.rows):
+                    block = feats[l][r, base : base + 8, p * LANES : p * LANES + w]
+                    side[slot, 9 * r : 9 * r + 8, 0:w] = block.astype(F32)
                 for i in range(n):
                     at = i + (8 - n if d == 0 else 0)
-                    value = side[6 * l + 3 * d + p, pl.ds(at, lv.rows, stride=8), 0:w]
+                    value = side[slot, pl.ds(at, lv.rows, stride=9), 0:w]
                     to[i, :, p * LANES : p * LANES + w] = value.astype(BF16)
 
     pl.semaphore_wait(barrier, count)
@@ -183,9 +192,9 @@
     scratch = [V(message(l0, (d, 0)), BF16) for d in (1, -1)]
     scratch += [V(message(lv, (0, d)), BF16) for lv in levels for d in (1, -1)]
     scratch += [
-        V((l0.chan * l0.rows, l0.cols), F32),
-        V((l0.rows * l0.cols, LANES), F32),
-        V((24, 8 * levels[1].rows, LANES), F32),
+        V((l0.chan * (l0.rows + 1), l0.cols), F32),
+        V((l0.rows * (l0.cols + 1), LANES), F32),
+        V((24, 9 * levels[1].rows, LANES), F32),
         pltpu.SemaphoreType.DMA((32,)),
         pltpu.SemaphoreType.DMA((32,)),
     ]
@@ -331,7 +340,10 @@
             run(i)
             return 0
 
-        lax.fori_loop(0, n, step, 0)
+        if n == 1:
+            run(0)
+        else:
+            lax.fori_loop(0, n, step, 0)
 
     def put(l, at, value):
         lv = levels[l]
@@ -421,10 +433,11 @@
         lv = levels[l]
         start, length = span
         n, m = chunking(length, 656)
+        group = GROUP if n % GROUP == 0 else 1
         C = lv.chan
 
-        def run(i):
-            base = pl.multiple_of(start + i * m, 8)
+        def run(i, j):
+            base = pl.multiple_of(start + (i * group + j) * m, 8)
             a, b, c = (
                 src[0, pl.ds(pl.multiple_of(base - 8 + d * lv.pitch, 8), m + 16), :] for d in (-1, 0, 1)
             )
@@ -438,14 +451,18 @@
                 lhs = jnp.concatenate([a.astype(BF16), b.astype(BF16), c.astype(BF16)], axis=1)
             o = lax.dot_general(lhs, weight[...], NT, preferred_element_type=F32)
             for q in range(3):
-                spread[q, 0 : m + 16, :] = o[:, q * LANES : (q + 1) * LANES]
-            y = spread[0, 7 : 7 + m, :] + spread[1, 8 : 8 + m, :] + spread[2, 9 : 9 + m, :]
+                spread[3 * j + q, 0 : m + 16, :] = o[:, q * LANES : (q + 1) * LANES]
+            y = spread[3 * j, 7 : 7 + m, :] + spread[3 * j + 1, 8 : 8 + m, :] + spread[3 * j + 2, 9 : 9 + m, :]
             y = y + bias
             if residual:
                 y = y + dst[0, pl.ds(base, m), :]
             dst[0, pl.ds(base, m), :] = jnp.maximum(y, 0.0)
 
-        rows_loop(n, run)
+        def several(i):
+            for j in range(group):
+                run(i, j)
+
+        rows_loop(n // group, several)
 
     def offset(lv, t):
         return (t // 3 - 1) * lv.pitch + t % 3 - 1
@@ -658,7 +675,7 @@
     m2, m3 = up_to(l2.first()[1], 16), up_to(l3.first()[1], 16)
     n1 = max(chunking(s[1], 656)[1] for lv in levels[:2] for s in (lv.first(), lv.second()))
     scratch = maps * 2 + [
-        V((3, n1 + 16, LANES), F32),
+        V((3 * GROUP, n1 + 16, LANES), F32),
         V((2, l2.total, LANES), F32),
         V((m2, 9 * c2), BF16),
         V((m3, 9 * c3), BF16),

time: 50.2 us -> 41.8 us (0.83)
  Pallas kernels: 46.5 us -> 38.1 us
    pallas_call x1, Pallas kernels: 17 us -> 11.9 us  [halos_of(): pl.pallas_call(functools.partial(exchange, levels), out_shape=shapes, in_...]
    pallas_call x1, Pallas kernels: 29.5 us -> 26.2 us  [per_device(): pl.pallas_call(functools.partial(body, levels), out_shape=[jax.ShapeDtype...]
where the time goes in v3:
time: 41.8 us; the launch traced here: 41.7 us
  Pallas kernels  38.1 us (91%)
  local copies, waits for them, and re-layouts  2.9 us (7%)
  between operations  0.65 us (2%)
    pallas_call x1, Pallas kernels, per_device(): pl.pallas_call(functools.partial(body, levels), out_shape=[jax.ShapeDtype...  26.2 us
    pallas_call x1, Pallas kernels, halos_of(): pl.pallas_call(functools.partial(exchange, levels), out_shape=shapes, in_...  11.9 us
    unnamed x1, local copies, waits for them, and re-layouts  2.9 us

profile of v3, /device:TPU:22, one launch (start us, length us, event | category | flops | bytes accessed | tf_op | source)
XLA Modules:
  0.0 41.7 jit_solution(17716417180657484690)
XLA Ops:
  0.6 11.9 %shard_map.219 = (bf16[2,8,128]{2,1,0:T(8,128)(2,1)}, bf16[2,32,128]{2,1,0:T(8,128)(2,1)}, bf16[9,8,128]{2,1,0:T(8,128)(2,1)}, bf16[2,32,128]{2,1,0:T(8,128)(2,1...) custom-call(bf16[48,64,64]{2,1,0:T(8,128)(2,1)} %refs_0_.1, ...), custom_call_target="tpu_custom_call" | custom-call | tf_op jit(solution)/shard_map/pallas_call | solution.py:201
  12.5 26.2 %shard_map.220 = (bf16[64,64,48]{2,1,0:T(8,128)(2,1)}, bf16[32,32,96]{2,1,0:T(8,128)(2,1)}, bf16[16,16,192]{2,1,0:T(8,128)(2,1)}, bf16[8,8,384]{2,1,0:T(8,128)(2,1)}) custom-call(bf16[64,64,48]{2,1,0:T(8,128)(2,1)} %get-tuple-element.41.refs_0_, bf16[32,32,96]{2,1,0:T(8,128)(2,1)} %bitcast.15, bf16[16,16,192]{2,1,0:T(8,128)(2,1)} %bitcast.19, ...), custom_call_target="tpu_custom_call" | custom-call | tf_op jit(solution)/shard_map/pallas_call | solution.py:702
  38.8 2.9 %copy.24 = bf16[48,64,64]{2,1,0:T(8,128)(2,1)} copy(bf16[48,64,64]{0,2,1:T(8,128)(2,1)} %bitcast.16) | data formatting | bytes 786432

commit v4 on v3

--- a/solution.py
+++ b/solution.py
@@ -218,48 +218,56 @@
     w0, w1, wd0, wd1a, wd1v, wd2, wd2v = made
     c0, c1, c2, c3 = (lv.chan for lv in levels)
 
-    def shifted(row, n, off, width, to):
+    def blank(ref, row, n, col, m):
+        ref[row : row + n, col : col + m] = jnp.zeros((n, m), BF16)
+
+    def shifted(ref, row, n, off, width, to):
+        def tile(k):
+            part = ref[row : row + n, k * LANES : min((k + 1) * LANES, ref.shape[1])].astype(F32)
+            if part.shape[1] < LANES:
+                part = jnp.concatenate([part, jnp.zeros((n, LANES - part.shape[1]), F32)], axis=1)
+            return part
+
         k, s = divmod(off, LANES)
-        a = stage[row : row + n, k * LANES : (k + 1) * LANES]
+        a = tile(k)
         ids = lax.broadcasted_iota(jnp.int32, a.shape, 1)
         if s + width > LANES:
-            a = jnp.where(ids >= s, a, stage[row : row + n, (k + 1) * LANES : (k + 2) * LANES])
+            a = jnp.where(ids >= s, a, tile(k + 1))
         if (to - s) % LANES:
             a = pltpu.roll(a, (to - s) % LANES, 1)
         if width == LANES:
             return a
         return jnp.where((ids >= to) & (ids < to + width), a, 0.0)
 
-    def fill(value):
-        n, k = value.shape
-        stage[0:n, 0:k] = value.astype(F32)
-
     for i in range(2):
-        fill(w0_in[i])
+        ref = w0_in.at[i]
         for q in range(3):
             offs = [c0 * (3 * p + q) for p in range(3)]
             cut = LANES - 2 * c0
-            tile = shifted(0, c0, offs[0], c0, 0) + shifted(0, c0, offs[1], c0, c0)
-            tile = tile + shifted(0, c0, offs[2], cut, 2 * c0)
+            tile = shifted(ref, 0, c0, offs[0], c0, 0) + shifted(ref, 0, c0, offs[1], c0, c0)
+            tile = tile + shifted(ref, 0, c0, offs[2], cut, 2 * c0)
             w0[i, q * LANES : q * LANES + c0, 0:LANES] = tile.astype(BF16)
-            tile = shifted(0, c0, offs[2] + cut, c0 - cut, 0)
+            tile = shifted(ref, 0, c0, offs[2] + cut, c0 - cut, 0)
             w0[i, q * LANES : q * LANES + c0, LANES : 2 * LANES] = tile.astype(BF16)
-        fill(w1_in[i])
+        ref = w1_in.at[i]
         for q in range(3):
+            blank(w1.at[i], q * LANES + c1, LANES - c1, 0, 3 * LANES)
             for p in range(3):
-                tile = shifted(0, c1, c1 * (3 * p + q), c1, 0)
+                tile = shifted(ref, 0, c1, c1 * (3 * p + q), c1, 0)
                 w1[i, q * LANES : q * LANES + c1, p * LANES : (p + 1) * LANES] = tile.astype(BF16)
 
-    def apart(value, to, row):
-        fill(value)
+    def apart(ref, first, to, row):
         for t in range(9):
-            to[row : row + c1, t * LANES : (t + 1) * LANES] = shifted(0, c1, c1 * t, c1, 0).astype(BF16)
-
+            tile = shifted(ref, first, c1, c1 * t, c1, 0)
+            to[row : row + c1, t * LANES : (t + 1) * LANES] = tile.astype(BF16)
+
+    blank(wd1a, c2, 2 * LANES - c2, 0, 9 * LANES)
+    blank(wd1a, 2 * LANES + c1, LANES - c1, 0, 9 * LANES)
     for k in range(c2 // c1):
-        apart(fin1[0, k * c1 : (k + 1) * c1, :], wd1a, k * c1)
-    apart(mid1[0, 0], wd1a, 2 * LANES)
+        apart(fin1.at[0], k * c1, wd1a, k * c1)
+    apart(mid1.at[0, 0], 0, wd1a, 2 * LANES)
     for k in range(c3 // c1):
-        apart(fin1[0, c2 + k * c1 : c2 + (k + 1) * c1, :], wd2v, k * c1)
+        apart(fin1.at[0], c2 + k * c1, wd2v, k * c1)
 
     tall = up_to(9 * c0, LANES)
 
@@ -273,21 +281,23 @@
     for t in range(9):
         wd0[t * LANES : t * LANES + c0, LANES : 2 * LANES] = flat[t * c0 : (t + 1) * c0, :]
         wd0[t * LANES : t * LANES + c0, 0:LANES] = fin0[t * c0 : (t + 1) * c0, 0:LANES]
+        blank(wd0, t * LANES + c0, LANES - c0, 0, 2 * LANES)
     stage[0:LANES, 0:tall] = jnp.zeros((LANES, tall), F32)
     stage[c2 - LANES : c2 - LANES + c0, 0 : 9 * c0] = mid0[0, 2].astype(F32)
     flat = turned()
     for t in range(9):
+        blank(wd1v, t * LANES + c0, c0, 0, LANES)
         wd1v[t * LANES + c0 : t * LANES + 2 * c0, LANES : 2 * LANES] = flat[t * c0 : (t + 1) * c0, :]
-    fill(fin0[...])
+        blank(wd1v, t * LANES + 2 * c0, LANES - 2 * c0, 0, 2 * LANES)
     depth = wd2.shape[0] // 9
     for t in range(9):
-        wd1v[t * LANES : t * LANES + c0, 0:LANES] = shifted(t * c0, c0, c1, LANES, 0).astype(BF16)
-        tile = shifted(t * c0, c0, c1 + LANES, c2 - LANES, 0)
+        wd1v[t * LANES : t * LANES + c0, 0:LANES] = shifted(fin0, t * c0, c0, c1, LANES, 0).astype(BF16)
+        tile = shifted(fin0, t * c0, c0, c1 + LANES, c2 - LANES, 0)
         wd1v[t * LANES : t * LANES + c0, LANES : 2 * LANES] = tile.astype(BF16)
         row = t * depth + c2
         wd2[row : row + depth - c2, :] = jnp.zeros((depth - c2, c3), BF16)
         for j in range(c3 // LANES):
-            tile = shifted(t * c0, c0, c1 + c2 + j * LANES, LANES, 0)
+            tile = shifted(fin0, t * c0, c0, c1 + c2 + j * LANES, LANES, 0)
             wd2[row : row + c0, j * LANES : (j + 1) * LANES] = tile.astype(BF16)
 
 
@@ -308,12 +318,12 @@
     spread, odd, cols2, cols3 = take(4)
     w2, w3 = take(2)
     w0, w1, wd0, wd1a, wd1v, wd2, wd2v, stage, bpad = take(9)
-    t01, v0, t2, v1, u0, u1, u2 = take(7)
+    t01, v0, t2, v1, u0, u1, u2, last = take(8)
     (sems,) = take(1)
     l0, l1, l2, l3 = levels
     copies = [pltpu.make_async_copy(a, b, sems.at[i]) for i, (a, b) in enumerate(((w2_hbm, w2), (w3_hbm, w3)))]
     depth = wd2.shape[0] // 9
-    for ref in (w0, w1, wd0, wd1a, wd1v, bpad):
+    for ref in (w0, bpad):
         ref[...] = jnp.zeros_like(ref)
     fin2_copies = [
         pltpu.make_async_copy(
@@ -349,12 +359,27 @@
         lv = levels[l]
         for p in range(lv.planes):
             w = min(LANES, lv.chan - p * LANES)
-            xs[l][p, pl.ds(at, value.shape[0]), 0:w] = value[:, p * LANES : p * LANES + w]
+            part = value[:, p * LANES : p * LANES + w]
+            if w < LANES:
+                part = jnp.concatenate([part, jnp.zeros((part.shape[0], LANES - w), F32)], axis=1)
+            xs[l][p, pl.ds(at, value.shape[0]), :] = part
 
     for l, lv in enumerate(levels):
-        xs[l][...] = jnp.zeros_like(xs[l])
-    for ref in (v0, v1):
-        ref[...] = jnp.zeros_like(ref)
+        for p in range(lv.planes):
+            for i in range(lv.lead + lv.rows + 2):
+                at = i * lv.pitch + lv.cols
+                xs[l][p, at : at + lv.tail, :] = jnp.zeros((lv.tail, LANES), F32)
+
+        @pl.when(top)
+        def _(l=l, lv=lv):
+            for p in range(lv.planes):
+                xs[l][p, 0 : lv.at(0) - lv.tail, :] = jnp.zeros((lv.at(0) - lv.tail, LANES), F32)
+
+        @pl.when(bottom)
+        def _(l=l, lv=lv):
+            for p in range(lv.planes):
+                xs[l][p, lv.at(lv.rows) : lv.total, :] = jnp.zeros((lv.total - lv.at(lv.rows), LANES), F32)
+
     for l, lv in enumerate(levels):
 
         def place(source, row, l=l, lv=lv):
@@ -550,7 +575,14 @@
         t01[0, pl.ds(at, 4 * l1.pitch), :] = o[:, 0:LANES]
         v0[0, pl.ds(at, 4 * l1.pitch), :] = jnp.maximum(o[:, LANES:], 0.0)
 
-    rows_loop(rows // 4, down0)
+    count = rows // 4
+    group = GROUP if count % GROUP == 0 else 1
+
+    def downs0(k):
+        for j in range(group):
+            down0(k * group + j)
+
+    rows_loop(count // group, downs0)
     blank(v0, l1, rim, 0)
 
     rows = l2.rows + 2
@@ -653,10 +685,17 @@
             for di in range(2):
                 i = 2 * (4 * k + r) + di
                 at = pl.multiple_of((i + l0.lead) * l0.pitch, 8)
-                total = xs[0][0, pl.ds(at, l0.cols), 0:c0] + up
-                outs[0][i, :, :] = jnp.maximum(total, 0.0).astype(BF16)
+                total = jnp.maximum(xs[0][0, pl.ds(at, l0.cols), 0:c0] + up, 0.0)
+                last[pl.ds(i, c0, stride=l0.rows + 1), :] = total.T
 
     rows_loop(l1.rows // 4, join1)
+
+    def leave(k):
+        for j in range(8):
+            at = pl.multiple_of(8 * k * (l0.rows + 1), 8) + j * (l0.rows + 1)
+            outs[0][8 * k + j] = last[pl.ds(at, l0.rows), :].astype(BF16)
+
+    rows_loop(c0 // 8, leave)
 
 
 def per_device(*args):
@@ -688,7 +727,7 @@
         V((9 * LANES, 2 * LANES), BF16),
         V((9 * up_to(c2, LANES), c3), BF16),
         V((c3, 9 * LANES), BF16),
-        V((up_to(9 * c0, 8), up_to(max(9 * c1, fin0.shape[1]), LANES) + LANES), F32),
+        V((LANES, up_to(9 * c0, LANES)), F32),
         V((2, 8, LANES), F32),
         V((1, l1.total, LANES), F32),
         V((1, l1.total, LANES), F32),
@@ -697,17 +736,19 @@
         V((1, l0.cols, LANES), F32),
         V((2, l1.rows * l1.cols, LANES), F32),
         V((4, l2.rows * l2.cols, LANES), F32),
+        V((c0 * (l0.rows + 1), l0.cols), F32),
         pltpu.SemaphoreType.DMA((11,)),
     ]
     outs = pl.pallas_call(
         functools.partial(body, levels),
-        out_shape=[jax.ShapeDtypeStruct(f.shape, BF16) for f in feats],
+        out_shape=[jax.ShapeDtypeStruct(args[0].shape, BF16)]
+        + [jax.ShapeDtypeStruct(f.shape, BF16) for f in feats[1:]],
         in_specs=[vmem] * 38 + [any_] * 2 + [vmem] * 11 + [any_],
         out_specs=[vmem] * 4,
         scratch_shapes=scratch,
         compiler_params=pltpu.CompilerParams(vmem_limit_bytes=60 * 2**20),
     )(*feats, *halos, *weights, *biases, up1, up2, up3, mid0, mid1, fin0, fin1, fin2)
-    return tuple(o.transpose(2, 0, 1) for o in outs)
+    return (outs[0], *(o.transpose(2, 0, 1) for o in outs[1:]))
 
 
 def solution(mesh):

time: 41.8 us -> 38.2 us (0.914)
  local copies, waits for them, and re-layouts: 2.9 us -> 0 us
  Pallas kernels: 38.1 us -> 37.4 us
    unnamed x1 -> x0, local copies, waits for them, and re-layouts: 2.9 us -> none
    pallas_call x1, Pallas kernels: 26.2 us -> 25.5 us  [per_device(): pl.pallas_call(functools.partial(body, levels), out_shape=[jax.ShapeDtype...]
where the time goes in v4:
time: 38.2 us; the launch traced here: 38 us
  Pallas kernels  37.4 us (98%)
  between operations  0.64 us (2%)
    pallas_call x1, Pallas kernels, per_device(): pl.pallas_call(functools.partial(body, levels), out_shape=[jax.ShapeDtype...  25.5 us
    pallas_call x1, Pallas kernels, halos_of(): pl.pallas_call(functools.partial(exchange, levels), out_shape=shapes, in_...  11.9 us

profile of v4, /device:TPU:22, one launch (start us, length us, event | category | flops | bytes accessed | tf_op | source)
XLA Modules:
  0.0 38.0 jit_solution(11425696327211625000)
XLA Ops:
  0.6 11.9 %shard_map.219 = (bf16[2,8,128]{2,1,0:T(8,128)(2,1)}, bf16[2,32,128]{2,1,0:T(8,128)(2,1)}, bf16[9,8,128]{2,1,0:T(8,128)(2,1)}, bf16[2,32,128]{2,1,0:T(8,128)(2,1...) custom-call(bf16[48,64,64]{2,1,0:T(8,128)(2,1)} %refs_0_.1, ...), custom_call_target="tpu_custom_call" | custom-call | tf_op jit(solution)/shard_map/pallas_call | solution.py:201
  12.5 25.5 %shard_map.220 = (bf16[48,64,64]{2,1,0:T(8,128)(2,1)}, bf16[32,32,96]{2,1,0:T(8,128)(2,1)}, bf16[16,16,192]{2,1,0:T(8,128)(2,1)}, bf16[8,8,384]{2,1,0:T(8,128)(2,1)}) custom-call(bf16[64,64,48]{2,1,0:T(8,128)(2,1)} %get-tuple-element.41.refs_0_, bf16[32,32,96]{2,1,0:T(8,128)(2,1)} %bitcast.14, bf16[16,16,192]{2,1,0:T(8,128)(2,1)} %bitcast.17, ...), custom_call_target="tpu_custom_call" | custom-call | tf_op jit(solution)/shard_map/pallas_call | solution.py:742

commit v5 on v4

--- a/solution.py
+++ b/solution.py
@@ -9,7 +9,9 @@
 
 RIMS = (7, 3, 1, 0)
 GROUP = 3
+MOST = 656
 LANES = 128
+HALF = 64
 NT = (((1,), (1,)), ((), ()))
 NN = (((1,), (0,)), ((), ()))
 WAYS = [(dy, dx) for dy in (-1, 0, 1) for dx in (-1, 0, 1) if dy or dx]
@@ -107,9 +109,10 @@
     def turn(i, _):
         for j in range(8):
             r = 8 * i + j
-            value = stage[pl.ds(r, C, stride=tall), :].T
+            value = stage[pl.ds(r, C, stride=tall), :]
+            value = jnp.concatenate([value, jnp.zeros((HALF - C, W), F32), value], axis=0).T
             at = pl.multiple_of(i * 8 * wide, 8) + j * wide
-            maps[pl.ds(at, W), 0:C] = value
+            maps[pl.ds(at, W), 0 : HALF + C] = value
             turned[r] = value.astype(BF16)
         return 0
 
@@ -118,7 +121,7 @@
     def folded(a, b):
         ids = lax.broadcasted_iota(jnp.int32, a.shape, 1)
         a, b = jnp.where(ids < C, a, 0.0), jnp.where(ids < C, b, 0.0)
-        return (a + pltpu.roll(b, LANES // 2, 1)).astype(BF16)
+        return (a + pltpu.roll(b, HALF, 1)).astype(BF16)
 
     half = W // 2
     for to, first, n in ((rows_sent[0], R - l0.low, l0.low), (rows_sent[1], 0, 2)):
@@ -187,7 +190,7 @@
     V = pltpu.VMEM
     l0 = levels[0]
     shapes = [jax.ShapeDtypeStruct(message(lv, way), BF16) for lv in levels for way in WAYS]
-    shapes.append(jax.ShapeDtypeStruct((l0.rows, l0.cols, l0.chan), BF16))
+    shapes.append(jax.ShapeDtypeStruct((l0.rows, l0.cols, HALF + l0.chan), BF16))
     vmem, hbm = pl.BlockSpec(memory_space=pltpu.VMEM), pl.BlockSpec(memory_space=pl.ANY)
     scratch = [V(message(l0, (d, 0)), BF16) for d in (1, -1)]
     scratch += [V(message(lv, (0, d)), BF16) for lv in levels for d in (1, -1)]
@@ -208,6 +211,11 @@
     )(*feats)
 
 
+def slot(t):
+    p, q = divmod(t, 3)
+    return (q, p) if p < 2 else (3 + q // 2, q % 2)
+
+
 def chunking(length, most):
     n = -(-length // most)
     return n, up_to(-(-length // n), 16)
@@ -239,22 +247,21 @@
             return a
         return jnp.where((ids >= to) & (ids < to + width), a, 0.0)
 
+    w0[...] = jnp.zeros_like(w0)
     for i in range(2):
-        ref = w0_in.at[i]
-        for q in range(3):
-            offs = [c0 * (3 * p + q) for p in range(3)]
-            cut = LANES - 2 * c0
-            tile = shifted(ref, 0, c0, offs[0], c0, 0) + shifted(ref, 0, c0, offs[1], c0, c0)
-            tile = tile + shifted(ref, 0, c0, offs[2], cut, 2 * c0)
-            w0[i, q * LANES : q * LANES + c0, 0:LANES] = tile.astype(BF16)
-            tile = shifted(ref, 0, c0, offs[2] + cut, c0 - cut, 0)
-            w0[i, q * LANES : q * LANES + c0, LANES : 2 * LANES] = tile.astype(BF16)
-        ref = w1_in.at[i]
-        for q in range(3):
-            blank(w1.at[i], q * LANES + c1, LANES - c1, 0, 3 * LANES)
-            for p in range(3):
-                tile = shifted(ref, 0, c1, c1 * (3 * p + q), c1, 0)
-                w1[i, q * LANES : q * LANES + c1, p * LANES : (p + 1) * LANES] = tile.astype(BF16)
+        for q, rows in ((0, (0,)), (2, (HALF,)), (1, (LANES, LANES + HALF))):
+            tile0 = shifted(w0_in.at[i], 0, c0, c0 * q, c0, 0) + shifted(w0_in.at[i], 0, c0, c0 * (3 + q), c0, HALF)
+            tile1 = shifted(w0_in.at[i], 0, c0, c0 * (6 + q), c0, 0)
+            for row in rows:
+                w0[i, row : row + c0, 0:LANES] = tile0.astype(BF16)
+                w0[i, row : row + c0, LANES : 2 * LANES] = tile1.astype(BF16)
+        for row in (0, LANES):
+            blank(w1.at[i], row + c1, LANES - c1, 0, 6 * LANES)
+        blank(w1.at[i], LANES, c1, 3 * LANES, 3 * LANES)
+        for p in range(3):
+            for q, row, col in ((0, 0, p), (2, 0, 3 + p), (1, LANES, p)):
+                tile = shifted(w1_in.at[i], 0, c1, c1 * (3 * p + q), c1, 0)
+                w1[i, row : row + c1, col * LANES : (col + 1) * LANES] = tile.astype(BF16)
 
     def apart(ref, first, to, row):
         for t in range(9):
@@ -279,9 +286,14 @@
         stage[k * c0 : (k + 1) * c0, 0 : 9 * c0] = mid0[0, k].astype(F32)
     flat = turned()
     for t in range(9):
-        wd0[t * LANES : t * LANES + c0, LANES : 2 * LANES] = flat[t * c0 : (t + 1) * c0, :]
-        wd0[t * LANES : t * LANES + c0, 0:LANES] = fin0[t * c0 : (t + 1) * c0, 0:LANES]
-        blank(wd0, t * LANES + c0, LANES - c0, 0, 2 * LANES)
+        k, half = slot(t)
+        row = k * LANES + half * HALF
+        wd0[row : row + c0, LANES : 2 * LANES] = flat[t * c0 : (t + 1) * c0, :]
+        wd0[row : row + c0, 0:LANES] = fin0[t * c0 : (t + 1) * c0, 0:LANES]
+    for k in range(5):
+        blank(wd0, k * LANES + c0, HALF - c0, 0, 2 * LANES)
+        n = HALF + c0 if k < 4 else HALF
+        blank(wd0, k * LANES + n, LANES - n, 0, 2 * LANES)
     stage[0:LANES, 0:tall] = jnp.zeros((LANES, tall), F32)
     stage[c2 - LANES : c2 - LANES + c0, 0 : 9 * c0] = mid0[0, 2].astype(F32)
     flat = turned()
@@ -323,8 +335,7 @@
     l0, l1, l2, l3 = levels
     copies = [pltpu.make_async_copy(a, b, sems.at[i]) for i, (a, b) in enumerate(((w2_hbm, w2), (w3_hbm, w3)))]
     depth = wd2.shape[0] // 9
-    for ref in (w0, bpad):
-        ref[...] = jnp.zeros_like(ref)
+    bpad[...] = jnp.zeros_like(bpad)
     fin2_copies = [
         pltpu.make_async_copy(
             fin2_hbm.at[pl.ds(t * l2.chan, l2.chan)], wd2.at[pl.ds(t * depth, l2.chan)], sems.at[2 + t]
@@ -337,6 +348,7 @@
     prepare(levels, (w0_in, w1_in, mid0, mid1, fin0, fin1), (w0, w1, wd0, wd1a, wd1v, wd2, wd2v), stage)
     for l in (0, 1):
         bpad[l, 0:2, 0 : levels[l].chan] = biases[l][...]
+    bpad[0, :, :] = bpad[0, :, :] + pltpu.roll(bpad[0, :, :], HALF, 1)
 
     ty, tx = lax.axis_index("ty"), lax.axis_index("tx")
     top, bottom = ty == 0, ty == lax.axis_size("ty") - 1
@@ -355,13 +367,22 @@
         else:
             lax.fori_loop(0, n, step, 0)
 
+    def unfolded(value):
+        value = value.astype(F32)
+        C, out = l0.chan, []
+        for v in (value, pltpu.roll(value, HALF, 1)):
+            v = jnp.where(lane(v.shape) < C, v, 0.0)
+            out.append(v + pltpu.roll(v, HALF, 1))
+        return out
+
     def put(l, at, value):
         lv = levels[l]
         for p in range(lv.planes):
             w = min(LANES, lv.chan - p * LANES)
-            part = value[:, p * LANES : p * LANES + w]
-            if w < LANES:
-                part = jnp.concatenate([part, jnp.zeros((part.shape[0], LANES - w), F32)], axis=1)
+            part = value if l == 0 else value[:, p * LANES : p * LANES + w]
+            if part.shape[1] < LANES:
+                pad = jnp.zeros((part.shape[0], LANES - part.shape[1]), F32)
+                part = jnp.concatenate([part, pad], axis=1)
             xs[l][p, pl.ds(at, value.shape[0]), :] = part
 
     for l, lv in enumerate(levels):
@@ -394,18 +415,14 @@
                 return place(source, row)
             half = lv.cols // 2
             for i in range(source.shape[0]):
-                value = source[i].astype(F32)
-                put(l, lv.at(row + i), value[:, : lv.chan])
-                put(l, lv.at(row + i, half), pltpu.roll(value, LANES // 2, 1)[:, : lv.chan])
+                for j, value in enumerate(unfolded(source[i])):
+                    put(l, lv.at(row + i, j * half), value)
 
         def place_cols(source, way, l=l, lv=lv):
             dy, dx = way
             for i in range(source.shape[0]):
                 col = i - lv.low if dx > 0 else lv.cols + i
-                value = source[i].astype(F32)
-                both = [value]
-                if lv.folds == 2:
-                    both = [value, pltpu.roll(value, LANES // 2, 1)]
+                both = [source[i].astype(F32)] if lv.folds == 1 else unfolded(source[i])
                 if dy > 0:
                     pieces = [(-lv.low, both[-1][lv.near - lv.low :])]
                 elif dy < 0:
@@ -416,8 +433,8 @@
                     for p in range(lv.planes):
                         w = min(LANES, lv.chan - p * LANES)
                         at = pl.ds(lv.at(row, col), v.shape[0], stride=lv.pitch)
-                        part = v[:, p * LANES : p * LANES + w]
-                        if w < LANES:
+                        part = v if lv.folds == 2 else v[:, p * LANES : p * LANES + w]
+                        if part.shape[1] < LANES:
                             part = jnp.concatenate([part, jnp.zeros((v.shape[0], LANES - w), F32)], axis=1)
                         xs[l][p, at, :] = part
 
@@ -454,30 +471,43 @@
 
         pl.when(top)(lambda: rows(-low, low))
 
+    def paired(piece):
+        tiles = [[], [], [], [], []]
+        for t in range(9):
+            tiles[slot(t)[0]].append(piece(t))
+        keep = lane(tiles[0][0].shape) < HALF
+        tiles = [jnp.where(keep, *tile) if len(tile) > 1 else tile[0] for tile in tiles]
+        return jnp.concatenate([tile.astype(BF16) for tile in tiles], axis=1)
+
     def wide_conv(l, src, dst, weight, bias, span, residual):
         lv = levels[l]
         start, length = span
-        n, m = chunking(length, 656)
+        n, m = chunking(length, MOST)
         group = GROUP if n % GROUP == 0 else 1
-        C = lv.chan
 
         def run(i, j):
             base = pl.multiple_of(start + (i * group + j) * m, 8)
-            a, b, c = (
-                src[0, pl.ds(pl.multiple_of(base - 8 + d * lv.pitch, 8), m + 16), :] for d in (-1, 0, 1)
-            )
-            if 3 * C <= 2 * LANES:
-                ids = lane(a.shape)
-                moved = pltpu.roll(c, 2 * C, 1)
-                tile0 = a + pltpu.roll(b, C, 1) + jnp.where(ids >= 2 * C, moved, 0.0)
-                tile1 = jnp.where(ids < 3 * C - LANES, moved, 0.0)
-                lhs = jnp.concatenate([tile0.astype(BF16), tile1.astype(BF16)], axis=1)
+
+            if l == 0:
+                a, b, c = (
+                    src[0, pl.ds(pl.multiple_of(base - 8 + d * lv.pitch, 8), m + 16), :] for d in (-1, 0, 1)
+                )
+                pieces = [jnp.where(lane(a.shape) < HALF, a, b), c]
             else:
-                lhs = jnp.concatenate([a.astype(BF16), b.astype(BF16), c.astype(BF16)], axis=1)
+                pieces = [
+                    src[0, pl.ds(base + d * lv.pitch + e, m + 16), :] for e in (-1, 1) for d in (-1, 0, 1)
+                ]
+            lhs = jnp.concatenate([piece.astype(BF16) for piece in pieces], axis=1)
             o = lax.dot_general(lhs, weight[...], NT, preferred_element_type=F32)
-            for q in range(3):
-                spread[3 * j + q, 0 : m + 16, :] = o[:, q * LANES : (q + 1) * LANES]
-            y = spread[3 * j, 7 : 7 + m, :] + spread[3 * j + 1, 8 : 8 + m, :] + spread[3 * j + 2, 9 : 9 + m, :]
+            one, two = spread.at[2 * j], spread.at[2 * j + 1]
+            one[0 : m + 16, :] = o[:, 0:LANES]
+            two[0 : m + 16, :] = o[:, LANES:]
+            if l == 0:
+                y = one[7 : 7 + m, :]
+                y = jnp.where(lane(y.shape) < HALF, y, one[9 : 9 + m, :])
+                y = y + pltpu.roll(y, HALF, 1) + two[8 : 8 + m, :]
+            else:
+                y = one[0:m, :] + two[1 : 1 + m, :]
             y = y + bias
             if residual:
                 y = y + dst[0, pl.ds(base, m), :]
@@ -566,11 +596,10 @@
 
     def down0(k):
         i0 = l1.rows - rows + 4 * k
-        taps = [
-            jnp.concatenate([gathered(xs[0], 0, l0, l1, i0 + r, t) for r in range(4)], axis=0).astype(BF16)
-            for t in range(9)
-        ]
-        o = lax.dot_general(jnp.concatenate(taps, axis=1), wd0[...], NN, preferred_element_type=F32)
+        taps = paired(
+            lambda t: jnp.concatenate([gathered(xs[0], 0, l0, l1, i0 + r, t) for r in range(4)], axis=0)
+        )
+        o = lax.dot_general(taps, wd0[...], NN, preferred_element_type=F32)
         at = pl.multiple_of((i0 + l1.lead) * l1.pitch - l1.tail, 8)
         t01[0, pl.ds(at, 4 * l1.pitch), :] = o[:, 0:LANES]
         v0[0, pl.ds(at, 4 * l1.pitch), :] = jnp.maximum(o[:, LANES:], 0.0)
@@ -712,17 +741,17 @@
     V = pltpu.VMEM
     maps = [V((lv.planes, lv.total, LANES), F32) for lv in levels]
     m2, m3 = up_to(l2.first()[1], 16), up_to(l3.first()[1], 16)
-    n1 = max(chunking(s[1], 656)[1] for lv in levels[:2] for s in (lv.first(), lv.second()))
+    most = max(chunking(s[1], MOST)[1] for lv in levels[:2] for s in (lv.first(), lv.second()))
     scratch = maps * 2 + [
-        V((3 * GROUP, n1 + 16, LANES), F32),
+        V((2 * GROUP, most + 16, LANES), F32),
         V((2, l2.total, LANES), F32),
         V((m2, 9 * c2), BF16),
         V((m3, 9 * c3), BF16),
         V(weights[2].shape, BF16),
         V(weights[3].shape, BF16),
-        V((2, 3 * LANES, 2 * LANES), BF16),
-        V((2, 3 * LANES, 3 * LANES), BF16),
-        V((9 * LANES, 2 * LANES), BF16),
+        V((2, 2 * LANES, 2 * LANES), BF16),
+        V((2, 2 * LANES, 6 * LANES), BF16),
+        V((5 * LANES, 2 * LANES), BF16),
         V((3 * LANES, 9 * LANES), BF16),
         V((9 * LANES, 2 * LANES), BF16),
         V((9 * up_to(c2, LANES), c3), BF16),

time: 38.2 us -> 36.2 us (0.948)
  Pallas kernels: 37.4 us -> 35.4 us
    pallas_call x1, Pallas kernels: 25.5 us -> 23.5 us  [per_device(): pl.pallas_call(functools.partial(body, levels), out_shape=[jax.ShapeDtype...]
where the time goes in v5:
time: 36.2 us; the launch traced here: 36 us
  Pallas kernels  35.4 us (98%)
  between operations  0.64 us (2%)
    pallas_call x1, Pallas kernels, per_device(): pl.pallas_call(functools.partial(body, levels), out_shape=[jax.ShapeDtype...  23.5 us
    pallas_call x1, Pallas kernels, halos_of(): pl.pallas_call(functools.partial(exchange, levels), out_shape=shapes, in_...  11.9 us

profile of v5, /device:TPU:22, one launch (start us, length us, event | category | flops | bytes accessed | tf_op | source)
XLA Modules:
  0.0 36.0 jit_solution(8888039454302823726)
XLA Ops:
  0.6 11.9 %shard_map.219 = (bf16[2,8,128]{2,1,0:T(8,128)(2,1)}, bf16[2,32,128]{2,1,0:T(8,128)(2,1)}, bf16[9,8,128]{2,1,0:T(8,128)(2,1)}, bf16[2,32,128]{2,1,0:T(8,128)(2,1...) custom-call(bf16[48,64,64]{2,1,0:T(8,128)(2,1)} %refs_0_.1, ...), custom_call_target="tpu_custom_call" | custom-call | tf_op jit(solution)/shard_map/pallas_call | solution.py:204
  12.5 23.5 %shard_map.220 = (bf16[48,64,64]{2,1,0:T(8,128)(2,1)}, bf16[32,32,96]{2,1,0:T(8,128)(2,1)}, bf16[16,16,192]{2,1,0:T(8,128)(2,1)}, bf16[8,8,384]{2,1,0:T(8,128)(2,1)}) custom-call(bf16[64,64,112]{2,1,0:T(8,128)(2,1)} %get-tuple-element.41.refs_0_, bf16[32,32,96]{2,1,0:T(8,128)(2,1)} %bitcast.14, bf16[16,16,192]{2,1,0:T(8,128)(2,1)} %bitcast.17, ...), custom_call_target="tpu_custom_call" | custom-call | tf_op jit(solution)/shard_map/pallas_call | solution.py:771

commit v6 on v5

--- a/solution.py
+++ b/solution.py
@@ -14,7 +14,7 @@
 HALF = 64
 NT = (((1,), (1,)), ((), ()))
 NN = (((1,), (0,)), ((), ()))
-WAYS = [(dy, dx) for dy in (-1, 0, 1) for dx in (-1, 0, 1) if dy or dx]
+WAYS = [(1, 1), (0, 1), (1, 0), (1, -1), (-1, 1), (0, -1), (-1, 0), (-1, -1)]
 F32, BF16 = jnp.float32, jnp.bfloat16
 
 
@@ -27,7 +27,7 @@
         self.rows, self.cols, self.chan = shape
         self.rim = RIMS[level]
         self.low = self.rim + 2
-        self.pitch = up_to(self.cols + 2 + self.low, 8)
+        self.pitch = up_to(self.cols + 2 + self.low, 8 if level < 3 else 4)
         self.lead = self.low + 1
         self.tail = self.pitch - self.cols
         self.planes = up_to(self.chan, LANES) // LANES
@@ -74,9 +74,13 @@
 
 
 def exchange(levels, *refs):
-    feats, outs, turned = refs[:4], refs[4:36], refs[36]
+    given, outs, turned = refs[:4], refs[4:36], refs[36]
     rows_sent, cols_sent = refs[37:39], refs[39:47]
-    stage, maps, side, send, recv = refs[47:]
+    stage, maps, side, send, recv, local = refs[47:53]
+    feats = refs[53:]
+    loads = [pltpu.make_async_copy(a, b, local.at[i]) for i, (a, b) in enumerate(zip(given, feats))]
+    for load_ in loads:
+        load_.start()
     here = {a: lax.axis_index(a) for a in ("ty", "tx")}
     barrier = pltpu.get_barrier_semaphore()
     l0 = levels[0]
@@ -95,6 +99,8 @@
         count = count + jnp.where(ok, 1, 0)
 
     C, R, W = l0.chan, l0.rows, l0.cols
+    for load_ in loads:
+        load_.wait()
 
     tall, wide = R + 1, W + 1
 
@@ -200,11 +206,13 @@
         V((24, 9 * levels[1].rows, LANES), F32),
         pltpu.SemaphoreType.DMA((32,)),
         pltpu.SemaphoreType.DMA((32,)),
+        pltpu.SemaphoreType.DMA((4,)),
     ]
+    scratch += [V(f.shape, BF16) for f in feats]
     return pl.pallas_call(
         functools.partial(exchange, levels),
         out_shape=shapes,
-        in_specs=[vmem] * 4,
+        in_specs=[hbm] * 4,
         out_specs=[hbm] * 32 + [vmem],
         scratch_shapes=scratch,
         compiler_params=pltpu.CompilerParams(collective_id=0, has_side_effects=True),
@@ -221,7 +229,7 @@
     return n, up_to(-(-length // n), 16)
 
 
-def prepare(levels, given, made, stage):
+def prepare(levels, given, made, stage, part):
     w0_in, w1_in, mid0, mid1, fin0, fin1 = given
     w0, w1, wd0, wd1a, wd1v, wd2, wd2v = made
     c0, c1, c2, c3 = (lv.chan for lv in levels)
@@ -247,34 +255,38 @@
             return a
         return jnp.where((ids >= to) & (ids < to + width), a, 0.0)
 
-    w0[...] = jnp.zeros_like(w0)
-    for i in range(2):
-        for q, rows in ((0, (0,)), (2, (HALF,)), (1, (LANES, LANES + HALF))):
-            tile0 = shifted(w0_in.at[i], 0, c0, c0 * q, c0, 0) + shifted(w0_in.at[i], 0, c0, c0 * (3 + q), c0, HALF)
-            tile1 = shifted(w0_in.at[i], 0, c0, c0 * (6 + q), c0, 0)
-            for row in rows:
-                w0[i, row : row + c0, 0:LANES] = tile0.astype(BF16)
-                w0[i, row : row + c0, LANES : 2 * LANES] = tile1.astype(BF16)
-        for row in (0, LANES):
-            blank(w1.at[i], row + c1, LANES - c1, 0, 6 * LANES)
-        blank(w1.at[i], LANES, c1, 3 * LANES, 3 * LANES)
-        for p in range(3):
-            for q, row, col in ((0, 0, p), (2, 0, 3 + p), (1, LANES, p)):
-                tile = shifted(w1_in.at[i], 0, c1, c1 * (3 * p + q), c1, 0)
-                w1[i, row : row + c1, col * LANES : (col + 1) * LANES] = tile.astype(BF16)
+    if part == 0:
+        w0[...] = jnp.zeros_like(w0)
+        for i in range(2):
+            for q, rows in ((0, (0,)), (2, (HALF,)), (1, (LANES, LANES + HALF))):
+                tile0 = shifted(w0_in.at[i], 0, c0, c0 * q, c0, 0) + shifted(w0_in.at[i], 0, c0, c0 * (3 + q), c0, HALF)
+                tile1 = shifted(w0_in.at[i], 0, c0, c0 * (6 + q), c0, 0)
+                for row in rows:
+                    w0[i, row : row + c0, 0:LANES] = tile0.astype(BF16)
+                    w0[i, row : row + c0, LANES : 2 * LANES] = tile1.astype(BF16)
+            for row in (0, LANES):
+                blank(w1.at[i], row + c1, LANES - c1, 0, 6 * LANES)
+            blank(w1.at[i], LANES, c1, 3 * LANES, 3 * LANES)
+            for p in range(3):
+                for q, row, col in ((0, 0, p), (2, 0, 3 + p), (1, LANES, p)):
+                    tile = shifted(w1_in.at[i], 0, c1, c1 * (3 * p + q), c1, 0)
+                    w1[i, row : row + c1, col * LANES : (col + 1) * LANES] = tile.astype(BF16)
+        return
 
     def apart(ref, first, to, row):
         for t in range(9):
             tile = shifted(ref, first, c1, c1 * t, c1, 0)
             to[row : row + c1, t * LANES : (t + 1) * LANES] = tile.astype(BF16)
 
-    blank(wd1a, c2, 2 * LANES - c2, 0, 9 * LANES)
-    blank(wd1a, 2 * LANES + c1, LANES - c1, 0, 9 * LANES)
-    for k in range(c2 // c1):
-        apart(fin1.at[0], k * c1, wd1a, k * c1)
-    apart(mid1.at[0, 0], 0, wd1a, 2 * LANES)
-    for k in range(c3 // c1):
-        apart(fin1.at[0], c2 + k * c1, wd2v, k * c1)
+    if part == 1:
+        blank(wd1a, c2, 2 * LANES - c2, 0, 9 * LANES)
+        blank(wd1a, 2 * LANES + c1, LANES - c1, 0, 9 * LANES)
+        for k in range(c2 // c1):
+            apart(fin1.at[0], k * c1, wd1a, k * c1)
+        apart(mid1.at[0, 0], 0, wd1a, 2 * LANES)
+        for k in range(c3 // c1):
+            apart(fin1.at[0], c2 + k * c1, wd2v, k * c1)
+        return
 
     tall = up_to(9 * c0, LANES)
 
@@ -324,28 +336,33 @@
     feats, halos = take(4), take(32)
     w0_in, w1_in, w2_hbm, w3_hbm = take(4)
     biases = take(4)
-    up1, up2, up3, mid0, mid1, fin0, fin1, fin2_hbm = take(8)
+    late, fin2_hbm = take(7), take(1)[0]
     outs = take(4)
     xs, hs = take(4), take(4)
     spread, odd, cols2, cols3 = take(4)
     w2, w3 = take(2)
+    up1, up2, up3, mid0, mid1, fin0, fin1 = arrived = take(7)
     w0, w1, wd0, wd1a, wd1v, wd2, wd2v, stage, bpad = take(9)
     t01, v0, t2, v1, u0, u1, u2, last = take(8)
     (sems,) = take(1)
     l0, l1, l2, l3 = levels
-    copies = [pltpu.make_async_copy(a, b, sems.at[i]) for i, (a, b) in enumerate(((w2_hbm, w2), (w3_hbm, w3)))]
+    pairs = [(w2_hbm, w2), (w3_hbm, w3), *zip(late, arrived)]
+    copies = [pltpu.make_async_copy(a, b, sems.at[i]) for i, (a, b) in enumerate(pairs)]
     depth = wd2.shape[0] // 9
     bpad[...] = jnp.zeros_like(bpad)
     fin2_copies = [
         pltpu.make_async_copy(
-            fin2_hbm.at[pl.ds(t * l2.chan, l2.chan)], wd2.at[pl.ds(t * depth, l2.chan)], sems.at[2 + t]
+            fin2_hbm.at[pl.ds(t * l2.chan, l2.chan)], wd2.at[pl.ds(t * depth, l2.chan)], sems.at[len(pairs) + t]
         )
         for t in range(9)
     ]
     for c in copies + fin2_copies:
         c.start()
 
-    prepare(levels, (w0_in, w1_in, mid0, mid1, fin0, fin1), (w0, w1, wd0, wd1a, wd1v, wd2, wd2v), stage)
+    ready = functools.partial(
+        prepare, levels, (w0_in, w1_in, mid0, mid1, fin0, fin1), (w0, w1, wd0, wd1a, wd1v, wd2, wd2v), stage
+    )
+    ready(0)
     for l in (0, 1):
         bpad[l, 0:2, 0 : levels[l].chan] = biases[l][...]
     bpad[0, :, :] = bpad[0, :, :] + pltpu.roll(bpad[0, :, :], HALF, 1)
@@ -404,11 +421,22 @@
     for l, lv in enumerate(levels):
 
         def place(source, row, l=l, lv=lv):
+            n = source.shape[0]
+            group = 8 if n % 8 == 0 else 1
+
             def run(i):
-                at = pl.multiple_of((i + row + lv.lead) * lv.pitch, 8)
-                put(l, at, source[i].astype(F32))
-
-            rows_loop(source.shape[0], run)
+                for j in range(group):
+                    k = i * group + j
+                    at = (k + row + lv.lead) * lv.pitch
+                    if not isinstance(i, int) and lv.pitch % 8 == 0:
+                        at = pl.multiple_of(at, 8)
+                    put(l, at, source[k].astype(F32))
+
+            if n % 8:
+                for i in range(n):
+                    run(i)
+            else:
+                rows_loop(n // 8, run)
 
         def place_rows(source, row, l=l, lv=lv):
             if lv.folds == 1:
@@ -464,7 +492,13 @@
                 size = n * lv.pitch
                 ref[p, pl.ds(lv.at(row) - lv.tail + 2, size), :] = jnp.zeros((size, LANES), F32)
 
-        pl.when(left)(lambda: columns(lv.pitch - low, low))
+        def before():
+            for p in range(planes):
+                for i in range(lv.lead - low - 1, lv.lead + lv.rows + high - 1):
+                    end = (i + 1) * lv.pitch
+                    ref[p, end - low : end, :] = jnp.zeros((low, LANES), F32)
+
+        pl.when(left)(before)
         if high:
             pl.when(right)(lambda: columns(lv.cols, high))
             pl.when(bottom)(lambda: rows(lv.rows, high))
@@ -568,23 +602,25 @@
                 part = part + dst[p, pl.ds(start, m), :]
             dst[p, pl.ds(start, m), :] = jnp.maximum(part, 0.0)
 
-    for l in (0, 1):
-        lv = levels[l]
-        wide_conv(l, xs[l], hs[l], (w0, w1)[l].at[0], bpad[l, 0:1, :], lv.first(), False)
-        blank(hs[l], lv, lv.rim + 1, 1)
-        wide_conv(l, hs[l], xs[l], (w0, w1)[l].at[1], bpad[l, 1:2, :], lv.second(), True)
-        blank(xs[l], lv, lv.rim, 0)
-
+    wide_conv(0, xs[0], hs[0], w0.at[0], bpad[0, 0:1, :], l0.first(), False)
+    blank(hs[0], l0, l0.rim + 1, 1)
+    wide_conv(0, hs[0], xs[0], w0.at[1], bpad[0, 1:2, :], l0.second(), True)
+    blank(xs[0], l0, l0.rim, 0)
+    for c in copies:
+        c.wait()
     hs[2][1, :, :] = jnp.zeros((l2.total, LANES), F32)
-    copies[0].wait()
+    wide_conv(1, xs[1], hs[1], w1.at[0], bpad[1, 0:1, :], l1.first(), False)
     deep_conv2(xs[2], hs[2], w2[0], biases[2][0:1, :], l2.first(), False)
-    blank(hs[2], l2, l2.rim + 1, 1)
+    deep_conv3(xs[3], hs[3], w3[0], biases[3][0:1, :], l3.first(), False)
+    ready(1)
+    for l in (1, 2, 3):
+        blank(hs[l], levels[l], levels[l].rim + 1, 1)
+    wide_conv(1, hs[1], xs[1], w1.at[1], bpad[1, 1:2, :], l1.second(), True)
     deep_conv2(hs[2], xs[2], w2[1], biases[2][1:2, :], l2.second(), True)
-    blank(xs[2], l2, l2.rim, 0)
-    copies[1].wait()
-    deep_conv3(xs[3], hs[3], w3[0], biases[3][0:1, :], l3.first(), False)
-    blank(hs[3], l3, 1, 1)
     deep_conv3(hs[3], xs[3], w3[1], biases[3][1:2, :], l3.second(), True)
+    ready(2)
+    for l in (1, 2):
+        blank(xs[l], levels[l], levels[l].rim, 0)
 
     def gathered(src, plane, big, small, i, t, width=None):
         width = small.pitch if width is None else width
@@ -749,6 +785,7 @@
         V((m3, 9 * c3), BF16),
         V(weights[2].shape, BF16),
         V(weights[3].shape, BF16),
+        *(V(r.shape, BF16) for r in (up1, up2, up3, mid0, mid1, fin0, fin1)),
         V((2, 2 * LANES, 2 * LANES), BF16),
         V((2, 2 * LANES, 6 * LANES), BF16),
         V((5 * LANES, 2 * LANES), BF16),
@@ -766,13 +803,13 @@
         V((2, l1.rows * l1.cols, LANES), F32),
         V((4, l2.rows * l2.cols, LANES), F32),
         V((c0 * (l0.rows + 1), l0.cols), F32),
-        pltpu.SemaphoreType.DMA((11,)),
+        pltpu.SemaphoreType.DMA((18,)),
     ]
     outs = pl.pallas_call(
         functools.partial(body, levels),
         out_shape=[jax.ShapeDtypeStruct(args[0].shape, BF16)]
         + [jax.ShapeDtypeStruct(f.shape, BF16) for f in feats[1:]],
-        in_specs=[vmem] * 38 + [any_] * 2 + [vmem] * 11 + [any_],
+        in_specs=[vmem] * 38 + [any_] * 2 + [vmem] * 4 + [any_] * 8,
         out_specs=[vmem] * 4,
         scratch_shapes=scratch,
         compiler_params=pltpu.CompilerParams(vmem_limit_bytes=60 * 2**20),

time: 36.2 us -> 31.3 us (0.86)
  Pallas kernels: 35.4 us -> 30.4 us
    pallas_call x1, Pallas kernels: 23.5 us -> 19.1 us  [per_device(): pl.pallas_call(functools.partial(body, levels), out_shape=[jax.ShapeDtype...]
    pallas_call x1, Pallas kernels: 11.9 us -> 11.3 us  [halos_of(): pl.pallas_call(functools.partial(exchange, levels), out_shape=shapes, in_...]
where the time goes in v6:
time: 31.3 us; the launch traced here: 31 us
  Pallas kernels  30.4 us (97%)
  between operations  0.64 us (2%)
    pallas_call x1, Pallas kernels, per_device(): pl.pallas_call(functools.partial(body, levels), out_shape=[jax.ShapeDtype...  19.1 us
    pallas_call x1, Pallas kernels, halos_of(): pl.pallas_call(functools.partial(exchange, levels), out_shape=shapes, in_...  11.3 us

profile of v6, /device:TPU:22, one launch (start us, length us, event | category | flops | bytes accessed | tf_op | source)
XLA Modules:
  0.0 31.0 jit_solution(7508667463796338815)
XLA Ops:
  0.6 11.3 %shard_map.219 = (bf16[9,16,128]{2,1,0:T(8,128)(2,1)}, bf16[9,32,128]{2,1,0:T(8,128)(2,1)}, bf16[9,32,128]{2,1,0:T(8,128)(2,1)}, bf16[2,16,128]{2,1,0:T(8,128)(2...) custom-call(bf16[48,64,64]{2,1,0:T(8,128)(2,1)} %refs_0_.1, ...), custom_call_target="tpu_custom_call" | custom-call | tf_op jit(solution)/shard_map/pallas_call | solution.py:212
  11.9 19.1 %shard_map.220 = (bf16[48,64,64]{2,1,0:T(8,128)(2,1)}, bf16[32,32,96]{2,1,0:T(8,128)(2,1)}, bf16[16,16,192]{2,1,0:T(8,128)(2,1)}, bf16[8,8,384]{2,1,0:T(8,128)(2,1)}) custom-call(bf16[64,64,112]{2,1,0:T(8,128)(2,1)} %get-tuple-element.41.refs_0_, bf16[32,32,96]{2,1,0:T(8,128)(2,1)} %bitcast.14, bf16[16,16,192]{2,1,0:T(8,128)(2,1)} %bitcast.17, ...), custom_call_target="tpu_custom_call" | custom-call | tf_op jit(solution)/shard_map/pallas_call | solution.py:808

commit v7 on v6

--- a/solution.py
+++ b/solution.py
@@ -1,4 +1,5 @@
 import functools
+import math
 
 import jax
 import jax.numpy as jnp
@@ -8,7 +9,7 @@
 from jax.sharding import PartitionSpec as P
 
 RIMS = (7, 3, 1, 0)
-GROUP = 3
+GROUP = 9
 MOST = 656
 LANES = 128
 HALF = 64
@@ -517,7 +518,7 @@
         lv = levels[l]
         start, length = span
         n, m = chunking(length, MOST)
-        group = GROUP if n % GROUP == 0 else 1
+        group = math.gcd(n, GROUP)
 
         def run(i, j):
             base = pl.multiple_of(start + (i * group + j) * m, 8)
@@ -602,19 +603,20 @@
                 part = part + dst[p, pl.ds(start, m), :]
             dst[p, pl.ds(start, m), :] = jnp.maximum(part, 0.0)
 
+    hs[2][1, :, :] = jnp.zeros((l2.total, LANES), F32)
     wide_conv(0, xs[0], hs[0], w0.at[0], bpad[0, 0:1, :], l0.first(), False)
-    blank(hs[0], l0, l0.rim + 1, 1)
-    wide_conv(0, hs[0], xs[0], w0.at[1], bpad[0, 1:2, :], l0.second(), True)
-    blank(xs[0], l0, l0.rim, 0)
+    wide_conv(1, xs[1], hs[1], w1.at[0], bpad[1, 0:1, :], l1.first(), False)
+    for l in (0, 1):
+        blank(hs[l], levels[l], levels[l].rim + 1, 1)
     for c in copies:
         c.wait()
-    hs[2][1, :, :] = jnp.zeros((l2.total, LANES), F32)
-    wide_conv(1, xs[1], hs[1], w1.at[0], bpad[1, 0:1, :], l1.first(), False)
     deep_conv2(xs[2], hs[2], w2[0], biases[2][0:1, :], l2.first(), False)
+    wide_conv(0, hs[0], xs[0], w0.at[1], bpad[0, 1:2, :], l0.second(), True)
     deep_conv3(xs[3], hs[3], w3[0], biases[3][0:1, :], l3.first(), False)
     ready(1)
-    for l in (1, 2, 3):
+    for l in (2, 3):
         blank(hs[l], levels[l], levels[l].rim + 1, 1)
+    blank(xs[0], l0, l0.rim, 0)
     wide_conv(1, hs[1], xs[1], w1.at[1], bpad[1, 1:2, :], l1.second(), True)
     deep_conv2(hs[2], xs[2], w2[1], biases[2][1:2, :], l2.second(), True)
     deep_conv3(hs[3], xs[3], w3[1], biases[3][1:2, :], l3.second(), True)
@@ -641,7 +643,7 @@
         v0[0, pl.ds(at, 4 * l1.pitch), :] = jnp.maximum(o[:, LANES:], 0.0)
 
     count = rows // 4
-    group = GROUP if count % GROUP == 0 else 1
+    group = math.gcd(count, GROUP)
 
     def downs0(k):
         for j in range(group):

time: 31.3 us -> 29.9 us (0.955)
  Pallas kernels: 30.4 us -> 29 us
    pallas_call x1, Pallas kernels: 19.1 us -> 17.7 us  [per_device(): pl.pallas_call(functools.partial(body, levels), out_shape=[jax.ShapeDtype...]
where the time goes in v7:
time: 29.9 us; the launch traced here: 29.6 us
  Pallas kernels  29 us (97%)
  between operations  0.64 us (2%)
    pallas_call x1, Pallas kernels, per_device(): pl.pallas_call(functools.partial(body, levels), out_shape=[jax.ShapeDtype...  17.7 us
    pallas_call x1, Pallas kernels, halos_of(): pl.pallas_call(functools.partial(exchange, levels), out_shape=shapes, in_...  11.3 us

profile of v7, /device:TPU:22, one launch (start us, length us, event | category | flops | bytes accessed | tf_op | source)
XLA Modules:
  0.0 29.6 jit_solution(16875937510327833001)
XLA Ops:
  0.6 11.3 %shard_map.219 = (bf16[9,16,128]{2,1,0:T(8,128)(2,1)}, bf16[9,32,128]{2,1,0:T(8,128)(2,1)}, bf16[9,32,128]{2,1,0:T(8,128)(2,1)}, bf16[2,16,128]{2,1,0:T(8,128)(2...) custom-call(bf16[48,64,64]{2,1,0:T(8,128)(2,1)} %refs_0_.1, ...), custom_call_target="tpu_custom_call" | custom-call | tf_op jit(solution)/shard_map/pallas_call | solution.py:213
  11.9 17.7 %shard_map.220 = (bf16[48,64,64]{2,1,0:T(8,128)(2,1)}, bf16[32,32,96]{2,1,0:T(8,128)(2,1)}, bf16[16,16,192]{2,1,0:T(8,128)(2,1)}, bf16[8,8,384]{2,1,0:T(8,128)(2,1)}) custom-call(bf16[64,64,112]{2,1,0:T(8,128)(2,1)} %get-tuple-element.41.refs_0_, bf16[32,32,96]{2,1,0:T(8,128)(2,1)} %bitcast.14, bf16[16,16,192]{2,1,0:T(8,128)(2,1)} %bitcast.17, ...), custom_call_target="tpu_custom_call" | custom-call | tf_op jit(solution)/shard_map/pallas_call | solution.py:810

commit v8 on v7

--- a/solution.py
+++ b/solution.py
@@ -114,16 +114,16 @@
     lax.fori_loop(0, C // 8, load, 0)
 
     def turn(i, _):
-        for j in range(8):
-            r = 8 * i + j
+        for j in range(16):
+            r = 16 * i + j
             value = stage[pl.ds(r, C, stride=tall), :]
             value = jnp.concatenate([value, jnp.zeros((HALF - C, W), F32), value], axis=0).T
-            at = pl.multiple_of(i * 8 * wide, 8) + j * wide
+            at = pl.multiple_of(i * 16 * wide, 8) + j * wide
             maps[pl.ds(at, W), 0 : HALF + C] = value
             turned[r] = value.astype(BF16)
         return 0
 
-    lax.fori_loop(0, R // 8, turn, 0)
+    lax.fori_loop(0, R // 16, turn, 0)
 
     def folded(a, b):
         ids = lax.broadcasted_iota(jnp.int32, a.shape, 1)
@@ -730,7 +730,7 @@
     enlarge(up2_0, u1, 0, c0, l2.rows, l2.cols)
     enlarge(up2_1, u1, 1, c1, l2.rows, l2.cols)
 
-    def join1(k):
+    def join1(k, slots):
         lines = []
         for r in range(4):
             i = 4 * k + r
@@ -747,15 +747,22 @@
         for r in range(4):
             line = y[r * l1.cols : (r + 1) * l1.cols, :]
             for dj in range(2):
-                u0[0, pl.ds(dj, l1.cols, stride=2), 0:c0] = line
-            up = u0[0, 0 : l0.cols, 0:c0]
+                u0[slots + r, pl.ds(dj, l1.cols, stride=2), 0:c0] = line
+            up = u0[slots + r, 0 : l0.cols, 0:c0]
             for di in range(2):
                 i = 2 * (4 * k + r) + di
                 at = pl.multiple_of((i + l0.lead) * l0.pitch, 8)
                 total = jnp.maximum(xs[0][0, pl.ds(at, l0.cols), 0:c0] + up, 0.0)
                 last[pl.ds(i, c0, stride=l0.rows + 1), :] = total.T
 
-    rows_loop(l1.rows // 4, join1)
+    count = l1.rows // 4
+    pair = math.gcd(count, 8)
+
+    def joins1(k):
+        for j in range(pair):
+            join1(k * pair + j, 4 * j)
+
+    rows_loop(count // pair, joins1)
 
     def leave(k):
         for j in range(8):
@@ -801,7 +808,7 @@
         V((1, l1.total, LANES), F32),
         V((2, (l2.rows + 2) * l2.pitch, LANES), F32),
         V((2, l2.total, LANES), F32),
-        V((1, l0.cols, LANES), F32),
+        V((32, l0.cols, LANES), F32),
         V((2, l1.rows * l1.cols, LANES), F32),
         V((4, l2.rows * l2.cols, LANES), F32),
         V((c0 * (l0.rows + 1), l0.cols), F32),

time: 29.9 us -> 27.9 us (0.933)
  Pallas kernels: 29 us -> 27 us
    pallas_call x1, Pallas kernels: 17.7 us -> 15.9 us  [per_device(): pl.pallas_call(functools.partial(body, levels), out_shape=[jax.ShapeDtype...]
where the time goes in v8:
time: 27.9 us; the launch traced here: 27.7 us
  Pallas kernels  27 us (97%)
  between operations  0.64 us (2%)
    pallas_call x1, Pallas kernels, per_device(): pl.pallas_call(functools.partial(body, levels), out_shape=[jax.ShapeDtype...  15.9 us
    pallas_call x1, Pallas kernels, halos_of(): pl.pallas_call(functools.partial(exchange, levels), out_shape=shapes, in_...  11.1 us

profile of v8, /device:TPU:22, one launch (start us, length us, event | category | flops | bytes accessed | tf_op | source)
XLA Modules:
  0.0 27.7 jit_solution(10400215356582809871)
XLA Ops:
  0.6 11.1 %shard_map.219 = (bf16[9,16,128]{2,1,0:T(8,128)(2,1)}, bf16[9,32,128]{2,1,0:T(8,128)(2,1)}, bf16[9,32,128]{2,1,0:T(8,128)(2,1)}, bf16[2,16,128]{2,1,0:T(8,128)(2...) custom-call(bf16[48,64,64]{2,1,0:T(8,128)(2,1)} %refs_0_.1, ...), custom_call_target="tpu_custom_call" | custom-call | tf_op jit(solution)/shard_map/pallas_call | solution.py:213
  11.7 15.9 %shard_map.220 = (bf16[48,64,64]{2,1,0:T(8,128)(2,1)}, bf16[32,32,96]{2,1,0:T(8,128)(2,1)}, bf16[16,16,192]{2,1,0:T(8,128)(2,1)}, bf16[8,8,384]{2,1,0:T(8,128)(2,1)}) custom-call(bf16[64,64,112]{2,1,0:T(8,128)(2,1)} %get-tuple-element.41.refs_0_, bf16[32,32,96]{2,1,0:T(8,128)(2,1)} %bitcast.14, bf16[16,16,192]{2,1,0:T(8,128)(2,1)} %bitcast.17, ...), custom_call_target="tpu_custom_call" | custom-call | tf_op jit(solution)/shard_map/pallas_call | solution.py:817
